TPU v7x, 32 devices: a whole 2x2x4 slice. The times are simulated.
32 devices in a mesh: dp: 8 (over y, x, core), tensor: 4 (over z).
Axes of the slice: x: 2, y: 2, z: 4, core: 2. Of those that a mesh axis runs over, the one named last changes fastest.
Arguments:
- tokens: bfloat16 [16, 577, 1024], P('dp', None, 'tensor'), may hold values from -6 to 6
- cotangent: float32 [16, 577, 1024], P('dp', None, 'tensor'), may hold values from -6 to 6
- image_counts: int32 [8], P('dp'), may hold values from 1 to 2, as said below
- w_qkv: float32 [2, 1024, 3, 1024], P(None, 'dp', None, 'tensor'), as said below
- w_out: float32 [2, 1024, 1024], P(None, 'dp', 'tensor'), may hold values from -0.75 to 0.75
- w_fc1: float32 [2, 1024, 4096], P(None, 'dp', 'tensor'), may hold values from -0.1875 to 0.1875
- w_fc2: float32 [2, 1024, 4096], P(None, 'dp', 'tensor'), may hold values from -0.09375 to 0.09375
- vec_small: float32 [2, 8, 1024], P(None, None, 'tensor'), as said below
- fc1_bias: float32 [2, 4096], P(None, 'tensor'), may hold values from -3 to 3
- mom_qkv: float32 [2, 2, 1024, 3, 1024], P(None, None, 'dp', None, 'tensor'), as said below
- mom_out: float32 [2, 2, 1024, 1024], P(None, None, 'dp', 'tensor'), as said below
- mom_fc1: float32 [2, 2, 1024, 4096], P(None, None, 'dp', 'tensor'), as said below
- mom_fc2: float32 [2, 2, 1024, 4096], P(None, None, 'dp', 'tensor'), as said below
- mom_vec: float32 [2, 2, 8, 1024], P(None, None, None, 'tensor'), as said below
- mom_bias: float32 [2, 2, 4096], P(None, None, 'tensor'), as said below
Outputs:
- output: float32 [16, 577, 1024], P('dp', None, 'tensor')
- input_grad: float32 [16, 577, 1024], P('dp', None, 'tensor')
- grad_qkv: float32 [2, 1024, 3, 1024], P(None, 'dp', None, 'tensor')
- grad_out: float32 [2, 1024, 1024], P(None, 'dp', 'tensor')
- grad_fc1: float32 [2, 1024, 4096], P(None, 'dp', 'tensor')
- grad_fc2: float32 [2, 1024, 4096], P(None, 'dp', 'tensor')
- grad_vec: float32 [2, 8, 1024], P(None, None, 'tensor')
- grad_bias: float32 [2, 4096], P(None, 'tensor')
- new_qkv: float32 [2, 1024, 3, 1024], P(None, 'dp', None, 'tensor')
- new_out: float32 [2, 1024, 1024], P(None, 'dp', 'tensor')
- new_fc1: float32 [2, 1024, 4096], P(None, 'dp', 'tensor')
- new_fc2: float32 [2, 1024, 4096], P(None, 'dp', 'tensor')
- new_vec: float32 [2, 8, 1024], P(None, None, 'tensor')
- new_bias: float32 [2, 4096], P(None, 'tensor')
- newmom_qkv: float32 [2, 2, 1024, 3, 1024], P(None, None, 'dp', None, 'tensor')
- newmom_out: float32 [2, 2, 1024, 1024], P(None, None, 'dp', 'tensor')
- newmom_fc1: float32 [2, 2, 1024, 4096], P(None, None, 'dp', 'tensor')
- newmom_fc2: float32 [2, 2, 1024, 4096], P(None, None, 'dp', 'tensor')
- newmom_vec: float32 [2, 2, 8, 1024], P(None, None, None, 'tensor')
- newmom_bias: float32 [2, 2, 4096], P(None, None, 'tensor')
Inputs may be any that keep to these rules, and one draw needn't show every extreme that they name: Every index of dp holds 1 or 2 images; some index holds 2 and some holds 1. Slot 2 i always holds an image, slot 2 i + 1 only where image_counts[i] is 2; other slots' tokens and cotangents are ignored. `w_qkv`: independent entries of mean 0 and deviation 1024^-0.5. `vec_small`: gains and shifts of order one. `mom_qkv`: second moments (index 1 of dimension 0) are positive. `mom_out`: second moments (index 1 of dimension 0) are positive. `mom_fc1`: second moments (index 1 of dimension 0) are positive. `mom_fc2`: second moments (index 1 of dimension 0) are positive. `mom_vec`: second moments (index 1 of dimension 0) are positive. `mom_bias`: second moments (index 1 of dimension 0) are positive.
All inputs are finite; a program needn't handle non-finite values.
Results may differ from a plain program's by a relative error of at most 0.022.
Values may be sent and summed in bfloat16 or wider, within the bound.
A program may use at most 256 MiB of HBM per device.

v0:
```python
import jax
import jax.numpy as jnp
from jax import lax
from jax.sharding import PartitionSpec as P

D = 1024
HEADS = 16
LAYERS = 2
STEP = 10


NORM_EPS = 1e-06
ROOT_HALF = 0.7071067811865476
INV_ROOT_TWO_PI = 0.3989422804014327
LEARN_RATE = 0.01
BETA_ONE = 0.9
BETA_TWO = 0.999
ADAM_EPS = 1e-08
WEIGHT_DECAY = 0.05
CONTRACT_LAST = (((1,), (1,)), ((), ()))
CONTRACT_FIRST = (((0,), (0,)), ((), ()))


def as_sent(shard):
    return jax.tree.map(lambda a: a.astype(jnp.bfloat16) if a.dtype == jnp.float32 else a, shard)


def gelu_value(preactivation):
    return 0.5 * preactivation * (1.0 + jax.scipy.special.erf(preactivation * ROOT_HALF))


def gelu_slope(preactivation):
    return (
        0.5 * (1.0 + jax.scipy.special.erf(preactivation * ROOT_HALF))
        + preactivation * jnp.exp(-0.5 * preactivation * preactivation) * INV_ROOT_TWO_PI
    )


def layer_statistics(hidden_state):
    totals = lax.psum(
        (jnp.sum(hidden_state, -1), jnp.sum(hidden_state * hidden_state, -1)), "tensor"
    )
    mean_row = totals[0][..., None] / D
    spread = totals[1][..., None] / D - mean_row * mean_row
    inv_std = lax.rsqrt(spread + NORM_EPS)
    return ((hidden_state - mean_row) * inv_std, inv_std)


def norm_back(d_normed, normed, inv_std, gain, carried):
    d_hat = d_normed * gain
    totals = lax.psum((jnp.sum(d_hat, -1), jnp.sum(d_hat * normed, -1)), "tensor")
    grad_in = carried + inv_std * (
        d_hat - totals[0][..., None] / D - normed * totals[1][..., None] / D
    )
    return (grad_in, jnp.sum(d_normed * normed, (0, 1)), jnp.sum(d_normed, (0, 1)))


def share_features(local_rows):
    return lax.all_gather(local_rows, "tensor", axis=2, tiled=True)


def sum_branch(partial_rows):
    return lax.psum_scatter(partial_rows, "tensor", scatter_dimension=2, tiled=True)


def share_grads(local_rows):
    return lax.all_gather(local_rows, "tensor", axis=2, tiled=True)


def sum_inputs(partial_rows):
    return lax.psum_scatter(
        partial_rows.astype(jnp.bfloat16), "tensor", scatter_dimension=2, tiled=True
    ).astype(jnp.float32)


def fetch_weights(w_qkv, w_out, w_fc1, w_fc2, layer_number):
    pieces = (
        w_qkv[layer_number].astype(jnp.bfloat16),
        w_out[layer_number].astype(jnp.bfloat16),
        w_fc1[layer_number].astype(jnp.bfloat16),
        w_fc2[layer_number].astype(jnp.bfloat16),
    )
    return (
        lax.all_gather(pieces[0], "dp", axis=0, tiled=True),
        lax.all_gather(pieces[1], "dp", axis=0, tiled=True),
        lax.all_gather(pieces[2], "dp", axis=0, tiled=True),
        lax.all_gather(pieces[3], "dp", axis=0, tiled=True),
    )


def attend_forward(query_h, key_h, value_h, attn_scale):
    scores = (
        jnp.einsum("bqhd,bkhd->bhqk", query_h, key_h, preferred_element_type=jnp.float32)
        * attn_scale
    )
    top_score = jnp.max(scores, -1, keepdims=True)
    logged_total = top_score + jnp.log(jnp.sum(jnp.exp(scores - top_score), -1, keepdims=True))
    probs = jnp.exp(scores - logged_total).astype(jnp.bfloat16)
    attention_result = jnp.einsum(
        "bhqk,bkhd->bqhd", probs, value_h, preferred_element_type=jnp.float32
    ).astype(jnp.bfloat16)
    return (attention_result, logged_total)


def attend_backward(query_h, key_h, value_h, attention_result, d_att, logged_total, attn_scale):
    scores = (
        jnp.einsum("bqhd,bkhd->bhqk", query_h, key_h, preferred_element_type=jnp.float32)
        * attn_scale
    )
    probs = jnp.exp(scores - logged_total)
    probs_low = probs.astype(jnp.bfloat16)
    d_value = jnp.einsum("bhqk,bqhd->bkhd", probs_low, d_att, preferred_element_type=jnp.float32)
    d_probs = jnp.einsum("bqhd,bkhd->bhqk", d_att, value_h, preferred_element_type=jnp.float32)
    delta = jnp.sum(d_att.astype(jnp.float32) * attention_result.astype(jnp.float32), -1)
    d_scores = (probs * (d_probs - jnp.swapaxes(delta, 1, 2)[..., None]) * attn_scale).astype(
        jnp.bfloat16
    )
    d_query = jnp.einsum("bhqk,bkhd->bqhd", d_scores, key_h, preferred_element_type=jnp.float32)
    d_key = jnp.einsum("bhqk,bqhd->bkhd", d_scores, query_h, preferred_element_type=jnp.float32)
    return (d_query, d_key, d_value)


def adam_update(param, running_gradient, moments, decay):
    first = BETA_ONE * moments[0] + (1.0 - BETA_ONE) * running_gradient
    second = BETA_TWO * moments[1] + (1.0 - BETA_TWO) * running_gradient * running_gradient
    fix_one = 1.0 - BETA_ONE**STEP
    fix_two = 1.0 - BETA_TWO**STEP
    update = first / fix_one / (jnp.sqrt(second / fix_two) + ADAM_EPS) + decay * param
    return (param - LEARN_RATE * update, jnp.stack([first, second]))


def on_device(
    tokens,
    cotangent,
    image_counts,
    w_qkv,
    w_out,
    w_fc1,
    w_fc2,
    vec_small,
    fc1_bias,
    mom_qkv,
    mom_out,
    mom_fc1,
    mom_fc2,
    mom_vec,
    mom_bias,
):
    slot_count, seq_len, feat_width = tokens.shape
    tok_rows = slot_count * seq_len
    heads_here = HEADS // lax.axis_size("tensor")
    head_dim = feat_width // heads_here
    attn_scale = head_dim ** (-0.5)
    slot_live = jnp.stack([jnp.ones((), jnp.float32), (image_counts[0] == 2).astype(jnp.float32)])[
        :, None, None
    ]

    def to_heads(matrix):
        return matrix.reshape(slot_count, seq_len, heads_here, head_dim)

    def to_slots(matrix):
        return matrix.reshape(slot_count, seq_len, -1)

    hidden_state = tokens.astype(jnp.float32)
    saved_tensors = []
    fetched = []
    for layer_number in range(LAYERS):
        weights = fetch_weights(w_qkv, w_out, w_fc1, w_fc2, layer_number)
        fetched.append(weights)
        projection_weight, backward_weight, first_weight, second_weight = weights
        vector_rows = vec_small[layer_number]
        first_centered_scaled, first_inverse_deviation = layer_statistics(hidden_state)
        first_normalized = share_features(
            (first_centered_scaled * vector_rows[0] + vector_rows[1]).astype(jnp.bfloat16)
        ).reshape(tok_rows, -1)
        proj_out = lax.dot_general(
            first_normalized,
            projection_weight,
            (((1,), (0,)), ((), ())),
            preferred_element_type=jnp.float32,
        )
        query_matrix_rows = (proj_out[:, 0] + vector_rows[2]).astype(jnp.bfloat16)
        key_matrix_rows = proj_out[:, 1].astype(jnp.bfloat16)
        value_matrix_rows = (proj_out[:, 2] + vector_rows[3]).astype(jnp.bfloat16)
        attention_result, logged_total = attend_forward(
            to_heads(query_matrix_rows),
            to_heads(key_matrix_rows),
            to_heads(value_matrix_rows),
            attn_scale,
        )
        attention_result = attention_result.reshape(tok_rows, feat_width)
        attn_branch = sum_branch(
            to_slots(
                lax.dot_general(
                    attention_result,
                    backward_weight,
                    CONTRACT_LAST,
                    preferred_element_type=jnp.float32,
                )
            )
        )
        middle_state = hidden_state + attn_branch + vector_rows[4]
        second_centered_scaled, second_inverse_deviation = layer_statistics(middle_state)
        second_normalized = share_features(
            (second_centered_scaled * vector_rows[5] + vector_rows[6]).astype(jnp.bfloat16)
        ).reshape(tok_rows, -1)
        preactivation = (
            jnp.dot(second_normalized, first_weight, preferred_element_type=jnp.float32)
            + fc1_bias[layer_number]
        )
        activation_narrow = gelu_value(preactivation).astype(jnp.bfloat16)
        branch_two = lax.dot_general(
            activation_narrow, second_weight, CONTRACT_LAST, preferred_element_type=jnp.float32
        )
        new_hidden = middle_state + sum_branch(to_slots(branch_two)) + vector_rows[7]
        saved_tensors.append(
            (
                first_centered_scaled,
                first_inverse_deviation,
                first_normalized,
                query_matrix_rows,
                key_matrix_rows,
                value_matrix_rows,
                attention_result,
                logged_total,
                second_centered_scaled,
                second_inverse_deviation,
                second_normalized,
                preactivation,
                activation_narrow,
            )
        )
        hidden_state = new_hidden
    output = hidden_state * slot_live
    running_gradient = cotangent * slot_live
    big_grads = [None] * LAYERS
    vec_grads = [None] * LAYERS
    bias_grads = [None] * LAYERS
    for layer_number in reversed(range(LAYERS)):
        projection_weight, backward_weight, first_weight, second_weight = fetch_weights(
            w_qkv, w_out, w_fc1, w_fc2, layer_number
        )
        vector_rows = vec_small[layer_number]
        (
            first_centered_scaled,
            first_inverse_deviation,
            first_normalized,
            query_matrix_rows,
            key_matrix_rows,
            value_matrix_rows,
            attention_result,
            logged_total,
            second_centered_scaled,
            second_inverse_deviation,
            second_normalized,
            preactivation,
            activation_narrow,
        ) = saved_tensors[layer_number]
        full_grad = share_grads(running_gradient.astype(jnp.bfloat16)).reshape(tok_rows, -1)
        g_fc2 = lax.dot_general(
            full_grad, activation_narrow, CONTRACT_FIRST, preferred_element_type=jnp.float32
        )
        g_bias_two = jnp.sum(running_gradient, (0, 1))
        d_pre = jnp.dot(full_grad, second_weight, preferred_element_type=jnp.float32) * gelu_slope(
            preactivation
        )
        d_pre_low = d_pre.astype(jnp.bfloat16)
        g_fc1 = lax.dot_general(
            second_normalized, d_pre_low, CONTRACT_FIRST, preferred_element_type=jnp.float32
        )
        g_fc1_bias = jnp.sum(d_pre, 0)
        second_normed_gradient = sum_inputs(
            to_slots(
                lax.dot_general(
                    d_pre_low, first_weight, CONTRACT_LAST, preferred_element_type=jnp.float32
                )
            )
        )
        middle_gradient, second_gain_gradient, second_shift_gradient = norm_back(
            second_normed_gradient,
            second_centered_scaled,
            second_inverse_deviation,
            vector_rows[5],
            running_gradient,
        )
        full_mid = share_grads(middle_gradient.astype(jnp.bfloat16)).reshape(tok_rows, -1)
        g_out = lax.dot_general(
            full_mid, attention_result, CONTRACT_FIRST, preferred_element_type=jnp.float32
        )
        g_bias_out = jnp.sum(middle_gradient, (0, 1))
        d_att = jnp.dot(full_mid, backward_weight, preferred_element_type=jnp.float32).astype(
            jnp.bfloat16
        )
        d_query, d_key, d_value = attend_backward(
            to_heads(query_matrix_rows),
            to_heads(key_matrix_rows),
            to_heads(value_matrix_rows),
            to_heads(attention_result),
            to_heads(d_att),
            logged_total,
            attn_scale,
        )
        d_query = d_query.reshape(tok_rows, feat_width)
        d_key = d_key.reshape(tok_rows, feat_width)
        d_value = d_value.reshape(tok_rows, feat_width)
        d_proj = jnp.stack([d_query, d_key, d_value], axis=1).astype(jnp.bfloat16)
        g_qkv = lax.dot_general(
            first_normalized, d_proj, CONTRACT_FIRST, preferred_element_type=jnp.float32
        )
        first_normed_gradient = sum_inputs(
            to_slots(
                lax.dot_general(
                    d_proj,
                    projection_weight,
                    (((1, 2), (1, 2)), ((), ())),
                    preferred_element_type=jnp.float32,
                )
            )
        )
        running_gradient, first_gain_gradient, first_shift_gradient = norm_back(
            first_normed_gradient,
            first_centered_scaled,
            first_inverse_deviation,
            vector_rows[0],
            middle_gradient,
        )
        vec_grads[layer_number] = jnp.stack(
            [
                first_gain_gradient,
                first_shift_gradient,
                jnp.sum(d_query, 0),
                jnp.sum(d_value, 0),
                g_bias_out,
                second_gain_gradient,
                second_shift_gradient,
                g_bias_two,
            ]
        )
        bias_grads[layer_number] = g_fc1_bias
        layer_tuple = (g_qkv, g_out, g_fc1, g_fc2)
        big_grads[layer_number] = layer_tuple
    input_grad = running_gradient * slot_live
    stacked = tuple((jnp.stack([entry[which] for entry in big_grads]) for which in range(4)))
    stacked = jax.tree.map(
        lambda part: part.astype(jnp.float32),
        lax.psum_scatter(as_sent(stacked), "dp", scatter_dimension=1, tiled=True),
    )
    small_sums = lax.psum((jnp.stack(vec_grads), jnp.stack(bias_grads)), "dp")
    grad_totals = (stacked[0], stacked[1], stacked[2], stacked[3], small_sums[0], small_sums[1])
    params = (w_qkv, w_out, w_fc1, w_fc2, vec_small, fc1_bias)
    moments = (mom_qkv, mom_out, mom_fc1, mom_fc2, mom_vec, mom_bias)
    decays = (WEIGHT_DECAY, WEIGHT_DECAY, WEIGHT_DECAY, WEIGHT_DECAY, 0.0, 0.0)
    results = [
        adam_update(param, grad_total, moment, decay)
        for param, grad_total, moment, decay in zip(params, grad_totals, moments, decays)
    ]
    return (
        output,
        input_grad,
        grad_totals[0],
        grad_totals[1],
        grad_totals[2],
        grad_totals[3],
        grad_totals[4],
        grad_totals[5],
        results[0][0],
        results[1][0],
        results[2][0],
        results[3][0],
        results[4][0],
        results[5][0],
        results[0][1],
        results[1][1],
        results[2][1],
        results[3][1],
        results[4][1],
        results[5][1],
    )


def solution(mesh):
    return jax.shard_map(
        on_device,
        mesh=mesh,
        in_specs=(
            P("dp", None, "tensor"),
            P("dp", None, "tensor"),
            P("dp"),
            P(None, "dp", None, "tensor"),
            P(None, "dp", "tensor"),
            P(None, "dp", "tensor"),
            P(None, "dp", "tensor"),
            P(None, None, "tensor"),
            P(None, "tensor"),
            P(None, None, "dp", None, "tensor"),
            P(None, None, "dp", "tensor"),
            P(None, None, "dp", "tensor"),
            P(None, None, "dp", "tensor"),
            P(None, None, None, "tensor"),
            P(None, None, "tensor"),
        ),
        out_specs=(
            P("dp", None, "tensor"),
            P("dp", None, "tensor"),
            P(None, "dp", None, "tensor"),
            P(None, "dp", "tensor"),
            P(None, "dp", "tensor"),
            P(None, "dp", "tensor"),
            P(None, None, "tensor"),
            P(None, "tensor"),
            P(None, "dp", None, "tensor"),
            P(None, "dp", "tensor"),
            P(None, "dp", "tensor"),
            P(None, "dp", "tensor"),
            P(None, None, "tensor"),
            P(None, "tensor"),
            P(None, None, "dp", None, "tensor"),
            P(None, None, "dp", "tensor"),
            P(None, None, "dp", "tensor"),
            P(None, None, "dp", "tensor"),
            P(None, None, None, "tensor"),
            P(None, None, "tensor"),
        ),
        check_vma=False,
    )
```

profile of v0, /device:TPU:0, one launch (start us, length us, event | category | flops | bytes accessed | tf_op | source)
XLA Modules:
  0.0 1668.8 jit_solution(3100951194035109462)
XLA Ops:
  9.8 20.6 %all-reduce.8 = (f32[2,577]{1,0:T(2,128)S(1)}, f32[2,577]{1,0:T(2,128)S(1)}) all-reduce(f32[2,577]{1,0:T(2,128)S(1)} %get-tuple-element.103, f32[2,577]{1,0:T(2,128)S(1)} %get-tuple-element.102), channel_id=1, replica_groups=mesh['dp'=8,'tensor'=4] {'tensor'}, use_global_device_ids=true, to_apply=%region_3.0 | all-reduce | flops 2308 | bytes 18464 | tf_op jit(solution)/shard_map/psum | solution.py:40
  33.9 9.9 all-gather.1
  43.8 38.4 %all-gather.23.cloned.1.call-done = bf16[2,577,1024]{2,1,0:T(8,128)(2,1)} async-done(((bf16[2,577,256]{2,1,0:T(8,128)(2,1)}), bf16[2,577,1024]{2,1,0:T(8,128)(2,1)}) %all-gather.23.cloned.1.call-update) | async-done | bytes 2363408 | tf_op jit(solution)/shard_map/all_gather | solution.py:59
  82.2 3.6 reshape.303
  85.7 22.7 %all-gather.39.cloned.1.call-done = bf16[1,1024,3,256]{3,1,2,0:T(8,128)(2,1)} async-done(((bf16[1,128,3,256]{3,1,2,0:T(8,128)(2,1)}), bf16[1,1024,3,256]{3,1,2,0:T(8,128)(2,1)}) %all-gather.39.cloned.1.call-update) | async-done | bytes 1572880 | tf_op jit(solution)/shard_map/all_gather | solution.py:84
  108.4 4.1 fusion.36
  128.2 3.9 multiply_reduce_fusion.1
  142.0 86.5 %reduce-scatter.13.cloned.1.call-done = f32[2,577,256]{2,1,0:T(8,128)} async-done(((f32[2,577,1024]{2,1,0:T(8,128)}), f32[2,577,256]{2,1,0:T(8,128)}) %reduce-scatter.13.cloned.1.call-update) | async-done | bytes 1181712 | tf_op jit(solution)/shard_map/reduce_scatter | solution.py:63
  230.3 18.0 %all-reduce.7 = (f32[2,577]{1,0:T(2,128)S(1)}, f32[2,577]{1,0:T(2,128)S(1)}) all-reduce(f32[2,577]{1,0:T(2,128)S(1)} %get-tuple-element.93, f32[2,577]{1,0:T(2,128)S(1)} %get-tuple-element.92), channel_id=1, replica_groups=mesh['dp'=8,'tensor'=4] {'tensor'}, use_global_device_ids=true, to_apply=%region_10.0 | all-reduce | flops 2308 | bytes 18464 | tf_op jit(solution)/shard_map/psum | solution.py:40
  253.2 45.9 %all-gather.25.cloned.1.call-done = bf16[2,577,1024]{2,1,0:T(8,128)(2,1)} async-done(((bf16[2,577,256]{2,1,0:T(8,128)(2,1)}), bf16[2,577,1024]{2,1,0:T(8,128)(2,1)}) %all-gather.25.cloned.1.call-update) | async-done | bytes 2363408 | tf_op jit(solution)/shard_map/all_gather | solution.py:59
  299.1 3.6 reshape.282
  302.7 24.7 %all-gather.41.cloned.1.call-done = bf16[1,1024,1024]{2,1,0:T(8,128)(2,1)} async-done(((bf16[1,128,1024]{2,1,0:T(8,128)(2,1)}), bf16[1,1024,1024]{2,1,0:T(8,128)(2,1)}) %all-gather.41.cloned.1.call-update) | async-done | bytes 2097168 | tf_op jit(solution)/shard_map/all_gather | solution.py:86
  327.4 7.1 multiply_convert_fusion.3
  334.5 23.0 %all-gather.43.cloned.1.call-done = bf16[1,1024,1024]{2,1,0:T(8,128)(2,1)} async-done(((bf16[1,128,1024]{2,1,0:T(8,128)(2,1)}), bf16[1,1024,1024]{2,1,0:T(8,128)(2,1)}) %all-gather.43.cloned.1.call-update) | async-done | bytes 2097168 | tf_op jit(solution)/shard_map/all_gather | solution.py:87
  357.5 7.1 fusion.16
  364.6 4.9 reshape.283
  369.6 86.5 %reduce-scatter.15.cloned.1.call-done = f32[2,577,256]{2,1,0:T(8,128)} async-done(((f32[2,577,1024]{2,1,0:T(8,128)}), f32[2,577,256]{2,1,0:T(8,128)}) %reduce-scatter.15.cloned.1.call-update) | async-done | bytes 1181712 | tf_op jit(solution)/shard_map/reduce_scatter | solution.py:63
  457.8 18.0 %all-reduce.6 = (f32[2,577]{1,0:T(2,128)S(1)}, f32[2,577]{1,0:T(2,128)S(1)}) all-reduce(f32[2,577]{1,0:T(2,128)S(1)} %get-tuple-element.91, f32[2,577]{1,0:T(2,128)S(1)} %get-tuple-element.90), channel_id=1, replica_groups=mesh['dp'=8,'tensor'=4] {'tensor'}, use_global_device_ids=true, to_apply=%region_15.0 | all-reduce | flops 2308 | bytes 18464 | tf_op jit(solution)/shard_map/psum | solution.py:40
  477.9 11.1 all-gather.5
  489.0 37.6 %all-gather.27.cloned.1.call-done = bf16[2,577,1024]{2,1,0:T(8,128)(2,1)} async-done(((bf16[2,577,256]{2,1,0:T(8,128)(2,1)}), bf16[2,577,1024]{2,1,0:T(8,128)(2,1)}) %all-gather.27.cloned.1.call-update) | async-done | bytes 2363408 | tf_op jit(solution)/shard_map/all_gather | solution.py:59
  530.1 22.7 %all-gather.45.cloned.1.call-done = bf16[1,1024,3,256]{3,1,2,0:T(8,128)(2,1)} async-done(((bf16[1,128,3,256]{3,1,2,0:T(8,128)(2,1)}), bf16[1,1024,3,256]{3,1,2,0:T(8,128)(2,1)}) %all-gather.45.cloned.1.call-update) | async-done | bytes 1572880 | tf_op jit(solution)/shard_map/all_gather | solution.py:84
  552.9 4.2 fusion.33
  590.9 83.4 %reduce-scatter.17.cloned.1.call-done = f32[2,577,256]{2,1,0:T(8,128)} async-done(((f32[2,577,1024]{2,1,0:T(8,128)}), f32[2,577,256]{2,1,0:T(8,128)}) %reduce-scatter.17.cloned.1.call-update) | async-done | bytes 1181712 | tf_op jit(solution)/shard_map/reduce_scatter | solution.py:63
  676.8 18.6 %all-reduce.5 = (f32[2,577]{1,0:T(2,128)S(1)}, f32[2,577]{1,0:T(2,128)S(1)}) all-reduce(f32[2,577]{1,0:T(2,128)S(1)} %get-tuple-element.89, f32[2,577]{1,0:T(2,128)S(1)} %get-tuple-element.88), channel_id=1, replica_groups=mesh['dp'=8,'tensor'=4] {'tensor'}, use_global_device_ids=true, to_apply=%region_22.0 | all-reduce | flops 2308 | bytes 18464 | tf_op jit(solution)/shard_map/psum | solution.py:40
  699.6 28.6 %all-gather.31.cloned.1.call-done = bf16[2,577,1024]{2,1,0:T(8,128)(2,1)} async-done(((bf16[2,577,256]{2,1,0:T(8,128)(2,1)}), bf16[2,577,1024]{2,1,0:T(8,128)(2,1)}) %all-gather.31.cloned.1.call-update) | async-done | bytes 2363408 | tf_op jit(solution)/shard_map/all_gather | solution.py:67
  731.7 47.8 %all-gather.29.cloned.1.call-done = bf16[2,577,1024]{2,1,0:T(8,128)(2,1)} async-done(((bf16[2,577,256]{2,1,0:T(8,128)(2,1)}), bf16[2,577,1024]{2,1,0:T(8,128)(2,1)}) %all-gather.29.cloned.1.call-update) | async-done | bytes 2363408 | tf_op jit(solution)/shard_map/all_gather | solution.py:59
  779.5 3.6 reshape.285
  783.0 24.9 %all-gather.47.cloned.1.call-done = bf16[1,1024,1024]{2,1,0:T(8,128)(2,1)} async-done(((bf16[1,128,1024]{2,1,0:T(8,128)(2,1)}), bf16[1,1024,1024]{2,1,0:T(8,128)(2,1)}) %all-gather.47.cloned.1.call-update) | async-done | bytes 2097168 | tf_op jit(solution)/shard_map/all_gather | solution.py:86
  807.9 7.2 multiply_convert_fusion.2
  815.1 22.9 %all-gather.49.cloned.1.call-done = bf16[1,1024,1024]{2,1,0:T(8,128)(2,1)} async-done(((bf16[1,128,1024]{2,1,0:T(8,128)(2,1)}), bf16[1,1024,1024]{2,1,0:T(8,128)(2,1)}) %all-gather.49.cloned.1.call-update) | async-done | bytes 2097168 | tf_op jit(solution)/shard_map/all_gather | solution.py:87
  838.1 7.1 fusion.135
  846.7 4.0 convolution_convert_fusion.1
  854.2 7.2 fusion.11
  861.5 5.0 reshape.286
  866.5 36.1 %reduce-scatter.21.cloned.1.call-done = bf16[2,577,256]{2,1,0:T(8,128)(2,1)} async-done(((bf16[2,577,1024]{2,1,0:T(8,128)(2,1)}), bf16[2,577,256]{2,1,0:T(8,128)(2,1)}) %reduce-scatter.21.cloned.1.call-update) | async-done | bytes 590864 | tf_op jit(solution)/shard_map/reduce_scatter | solution.py:71
  904.8 18.0 %all-reduce.4 = (f32[2,577]{1,0:T(2,128)S(1)}, f32[2,577]{1,0:T(2,128)S(1)}) all-reduce(f32[2,577]{1,0:T(2,128)S(1)} %get-tuple-element.83, f32[2,577]{1,0:T(2,128)S(1)} %get-tuple-element.96), channel_id=1, replica_groups=mesh['dp'=8,'tensor'=4] {'tensor'}, use_global_device_ids=true, to_apply=%region_28.0 | all-reduce | flops 2308 | bytes 18464 | tf_op jit(solution)/shard_map/psum | solution.py:51
  922.9 68.0 %reduce-scatter.19.cloned.1.call-done = f32[2,577,256]{2,1,0:T(8,128)} async-done(((f32[2,577,1024]{2,1,0:T(8,128)}), f32[2,577,256]{2,1,0:T(8,128)}) %reduce-scatter.19.cloned.1.call-update) | async-done | bytes 1181712 | tf_op jit(solution)/shard_map/reduce_scatter | solution.py:63
  996.3 51.5 %all-gather.33.cloned.1.call-done = bf16[2,577,1024]{2,1,0:T(8,128)(2,1)} async-done(((bf16[2,577,256]{2,1,0:T(8,128)(2,1)}), bf16[2,577,1024]{2,1,0:T(8,128)(2,1)}) %all-gather.33.cloned.1.call-update) | async-done | bytes 2363408 | tf_op jit(solution)/shard_map/all_gather | solution.py:67
  1061.8 8.6 multiply_convert_fusion.1
  1100.5 4.9 bitcast_convert_fusion.1
  1105.4 3.6 convert_element_type.243
  1109.0 46.6 %reduce-scatter.23.cloned.1.call-done = bf16[2,577,256]{2,1,0:T(8,128)(2,1)} async-done(((bf16[2,577,1024]{2,1,0:T(8,128)(2,1)}), bf16[2,577,256]{2,1,0:T(8,128)(2,1)}) %reduce-scatter.23.cloned.1.call-update) | async-done | bytes 590864 | tf_op jit(solution)/shard_map/reduce_scatter | solution.py:71
  1157.4 17.3 %all-reduce.3 = (f32[2,577]{1,0:T(2,128)S(1)}, f32[2,577]{1,0:T(2,128)S(1)}) all-reduce(f32[2,577]{1,0:T(2,128)S(1)} %get-tuple-element.85, f32[2,577]{1,0:T(2,128)S(1)} %get-tuple-element.95), channel_id=1, replica_groups=mesh['dp'=8,'tensor'=4] {'tensor'}, use_global_device_ids=true, to_apply=%region_34.0 | all-reduce | flops 2308 | bytes 18464 | tf_op jit(solution)/shard_map/psum | solution.py:51
  1179.2 49.1 %all-gather.35.cloned.1.call-done = bf16[2,577,1024]{2,1,0:T(8,128)(2,1)} async-done(((bf16[2,577,256]{2,1,0:T(8,128)(2,1)}), bf16[2,577,1024]{2,1,0:T(8,128)(2,1)}) %all-gather.35.cloned.1.call-update) | async-done | bytes 2363408 | tf_op jit(solution)/shard_map/all_gather | solution.py:67
  1231.8 7.1 fusion.136
  1240.4 3.9 convolution_convert_fusion
  1244.3 3.6 convert_element_type.248
  1248.0 46.6 %reduce-scatter.25.cloned.1.call-done = bf16[2,577,256]{2,1,0:T(8,128)(2,1)} async-done(((bf16[2,577,1024]{2,1,0:T(8,128)(2,1)}), bf16[2,577,256]{2,1,0:T(8,128)(2,1)}) %reduce-scatter.25.cloned.1.call-update) | async-done | bytes 590864 | tf_op jit(solution)/shard_map/reduce_scatter | solution.py:71
  1296.9 17.3 %all-reduce.2 = (f32[2,577]{1,0:T(2,128)S(1)}, f32[2,577]{1,0:T(2,128)S(1)}) all-reduce(f32[2,577]{1,0:T(2,128)S(1)} %get-tuple-element.81, f32[2,577]{1,0:T(2,128)S(1)} %get-tuple-element.97), channel_id=1, replica_groups=mesh['dp'=8,'tensor'=4] {'tensor'}, use_global_device_ids=true, to_apply=%region_39.0 | all-reduce | flops 2308 | bytes 18464 | tf_op jit(solution)/shard_map/psum | solution.py:51
  1318.8 5.5 convert_bitcast_fusion.2
  1330.0 5.5 convert_bitcast_fusion
  1349.0 3.6 fusion.39
  1352.6 15.1 all-gather.37.cloned.1.call-done
  1380.4 6.8 multiply_convert_fusion
  1389.8 7.4 fusion.125
  1397.3 4.0 fusion.126
  1414.7 4.9 bitcast_convert_fusion
  1419.5 3.6 convert_element_type.256
  1432.5 42.3 %reduce-scatter.35.cloned.1.call-done = bf16[2,128,1024]{2,1,0:T(8,128)(2,1)} async-done(((bf16[2,1024,1024]{2,1,0:T(8,128)(2,1)}), bf16[2,128,1024]{2,1,0:T(8,128)(2,1)}) %reduce-scatter.35.cloned.1.call-update) | async-done | bytes 524304 | tf_op jit(solution)/shard_map/reduce_scatter | solution.py:346
  1479.6 34.9 %reduce-scatter.31.cloned.1.call-done = bf16[2,128,256]{2,1,0:T(8,128)(2,1)} async-done(((bf16[2,1024,256]{2,1,0:T(8,128)(2,1)}), bf16[2,128,256]{2,1,0:T(8,128)(2,1)}) %reduce-scatter.31.cloned.1.call-update) | async-done | bytes 131088 | tf_op jit(solution)/shard_map/reduce_scatter | solution.py:346
  1517.2 46.7 %reduce-scatter.29.cloned.1.call-done = bf16[2,128,3,256]{3,1,2,0:T(8,128)(2,1)} async-done(((bf16[2,1024,3,256]{3,1,2,0:T(8,128)(2,1)}), bf16[2,128,3,256]{3,1,2,0:T(8,128)(2,1)}) %reduce-scatter.29.cloned.1.call-update) | async-done | bytes 393232 | tf_op jit(solution)/shard_map/reduce_scatter | solution.py:346
  1567.8 46.5 %reduce-scatter.27.cloned.1.call-done = bf16[2,577,256]{2,1,0:T(8,128)(2,1)} async-done(((bf16[2,577,1024]{2,1,0:T(8,128)(2,1)}), bf16[2,577,256]{2,1,0:T(8,128)(2,1)}) %reduce-scatter.27.cloned.1.call-update) | async-done | bytes 590864 | tf_op jit(solution)/shard_map/reduce_scatter | solution.py:71
  1616.3 17.2 %all-reduce.1 = (f32[2,577]{1,0:T(2,128)S(1)}, f32[2,577]{1,0:T(2,128)S(1)}) all-reduce(f32[2,577]{1,0:T(2,128)S(1)} %get-tuple-element.87, f32[2,577]{1,0:T(2,128)S(1)} %get-tuple-element.94), channel_id=1, replica_groups=mesh['dp'=8,'tensor'=4] {'tensor'}, use_global_device_ids=true, to_apply=%region_45.0 | all-reduce | flops 2308 | bytes 18464 | tf_op jit(solution)/shard_map/psum | solution.py:51
  1637.1 22.4 %all-reduce = (f32[2,8,256]{2,1,0:T(8,128)S(1)}, f32[2,1024]{1,0:T(2,128)S(1)}) all-reduce(f32[2,8,256]{2,1,0:T(8,128)S(1)} %pad_maximum_fusion.9, f32[2,1024]{1,0:T(2,128)S(1)} %pad_maximum_fusion.11), channel_id=1, replica_groups=mesh['dp'=8,'tensor'=4] {'dp'}, use_global_device_ids=true, to_apply=%region_66.0 | all-reduce | flops 6144 | bytes 49152 | tf_op jit(solution)/shard_map/psum | solution.py:348
  (365 shorter events, 239.8 us)
Async XLA Ops:
  7.2 25.6 %copy-start.30 = (f32[2,128,3,256]{3,1,2,0:T(8,128)S(1)}, f32[2,128,3,256]{3,1,2,0:T(8,128)}, u32[]{:S(2)}) copy-start(f32[2,128,3,256]{3,1,2,0:T(8,128)} %param.18) | copy-start | bytes 2359300
  7.2 75.0 %all-gather.23.cloned.1.call-start = ((), (), s32[]{:S(2)}) async-start(), calls=%async_computation.12 | async-start | bytes 2990080 | tf_op jit(solution)/shard_map/all_gather | solution.py:59
  8.3 24.4 %copy-start.65 = (f32[1,1,256]{2,1,0:T(1,128)}, f32[1,1,256]{2,1,0:T(1,128)S(1)}, u32[]{:S(2)}) copy-start(f32[1,1,256]{2,1,0:T(1,128)S(1)} %get-tuple-element.194) | copy-start | bytes 3076
  9.8 24.1 %copy-start.43 = (f32[2,128,256]{2,1,0:T(8,128)S(1)}, f32[2,128,256]{2,1,0:T(8,128)}, u32[]{:S(2)}) copy-start(f32[2,128,256]{2,1,0:T(8,128)} %param.19) | copy-start | bytes 786436
  32.7 75.7 %all-gather.39.cloned.1.call-start = ((), (), s32[]{:S(2)}) async-start(), calls=%async_computation.32 | async-start | bytes 1769472 | tf_op jit(solution)/shard_map/all_gather | solution.py:84
  33.6 194.8 %reduce-scatter.13.cloned.1.call-start = ((), (), s32[]{:S(2)}) async-start(), calls=%async_computation.13 | async-start | bytes 5980160 | tf_op jit(solution)/shard_map/reduce_scatter | solution.py:63
  33.8 94.4 %copy-start.56 = (f32[4,64]{1,0:T(4,128)}, f32[4,64]{1,0:T(4,128)S(1)}, u32[]{:S(2)}) copy-start(f32[4,64]{1,0:T(4,128)S(1)} %add.365) | copy-start | bytes 3076
  33.9 100.3 %copy-start.58 = (f32[4,64]{1,0:T(4,128)}, f32[4,64]{1,0:T(4,128)S(1)}, u32[]{:S(2)}) copy-start(f32[4,64]{1,0:T(4,128)S(1)} %add.362) | copy-start | bytes 3076
  43.8 95.1 %copy-start.37 = (bf16[1,1024,256]{2,1,0:T(8,128)(2,1)}, bf16[1,1024,256]{2,1,0:T(8,128)(2,1)S(1)}, u32[]{:S(2)}) copy-start(bf16[1,1024,256]{2,1,0:T(8,128)(2,1)S(1)} %all-gather.1) | copy-start | bytes 1572868
  117.3 10.9 copy-start.18
  128.2 6.0 copy-start.7
  141.9 86.5 %copy-start.5 = (bf16[2,577,256]{2,0,1:T(2,128)(2,1)S(1)}, bf16[2,577,256]{2,0,1:T(2,128)(2,1)}, u32[]{:S(2)}) copy-start(bf16[2,577,256]{2,0,1:T(2,128)(2,1)} %param.15) | copy-start | bytes 1772548
  142.0 157.1 %all-gather.25.cloned.1.call-start = ((), (), s32[]{:S(2)}) async-start(), calls=%async_computation.14 | async-start | bytes 2990080 | tf_op jit(solution)/shard_map/all_gather | solution.py:59
  228.5 21.1 %copy-start.27 = (f32[2,128,1024]{2,1,0:T(8,128)S(1)}, f32[2,128,1024]{2,1,0:T(8,128)}, u32[]{:S(2)}) copy-start(f32[2,128,1024]{2,1,0:T(8,128)} %param.20) | copy-start | bytes 3145732
  249.5 77.9 %all-gather.41.cloned.1.call-start = ((), (), s32[]{:S(2)}) async-start(), calls=%async_computation.33 | async-start | bytes 2359296 | tf_op jit(solution)/shard_map/all_gather | solution.py:86
  250.5 107.0 %all-gather.43.cloned.1.call-start = ((), (), s32[]{:S(2)}) async-start(), calls=%async_computation.34 | async-start | bytes 2359296 | tf_op jit(solution)/shard_map/all_gather | solution.py:87
  252.7 203.4 %reduce-scatter.15.cloned.1.call-start = ((), (), s32[]{:S(2)}) async-start(), calls=%async_computation.15 | async-start | bytes 5980160 | tf_op jit(solution)/shard_map/reduce_scatter | solution.py:63
  369.6 157.0 %all-gather.27.cloned.1.call-start = ((), (), s32[]{:S(2)}) async-start(), calls=%async_computation.16 | async-start | bytes 2990080 | tf_op jit(solution)/shard_map/all_gather | solution.py:59
  477.0 75.9 %all-gather.45.cloned.1.call-start = ((), (), s32[]{:S(2)}) async-start(), calls=%async_computation.35 | async-start | bytes 1769472 | tf_op jit(solution)/shard_map/all_gather | solution.py:84
  477.7 196.6 %reduce-scatter.17.cloned.1.call-start = ((), (), s32[]{:S(2)}) async-start(), calls=%async_computation.17 | async-start | bytes 5980160 | tf_op jit(solution)/shard_map/reduce_scatter | solution.py:63
  562.1 12.3 copy-start.20
  587.8 140.3 %all-gather.31.cloned.1.call-start = ((), (), s32[]{:S(2)}) async-start(), calls=%async_computation.20 | async-start | bytes 2990080 | tf_op jit(solution)/shard_map/all_gather | solution.py:67
  588.6 402.3 %copy-start.68 = (f32[2]{0:T(128)}, f32[2]{0:T(128)S(1)}, u32[]{:S(2)}) copy-start(f32[2]{0:T(128)S(1)} %add_convert_fusion.15) | copy-start | bytes 28
  590.9 188.6 %all-gather.29.cloned.1.call-start = ((), (), s32[]{:S(2)}) async-start(), calls=%async_computation.18 | async-start | bytes 2990080 | tf_op jit(solution)/shard_map/all_gather | solution.py:59
  698.0 110.0 %all-gather.47.cloned.1.call-start = ((), (), s32[]{:S(2)}) async-start(), calls=%async_computation.36 | async-start | bytes 2359296 | tf_op jit(solution)/shard_map/all_gather | solution.py:86
  698.7 139.3 %all-gather.49.cloned.1.call-start = ((), (), s32[]{:S(2)}) async-start(), calls=%async_computation.37 | async-start | bytes 2359296 | tf_op jit(solution)/shard_map/all_gather | solution.py:87
  699.3 203.3 %reduce-scatter.21.cloned.1.call-start = ((), (), s32[]{:S(2)}) async-start(), calls=%async_computation.21 | async-start | bytes 2990080 | tf_op jit(solution)/shard_map/reduce_scatter | solution.py:71
  838.1 8.6 copy-start.75
  854.2 136.7 %reduce-scatter.19.cloned.1.call-start = ((), (), s32[]{:S(2)}) async-start(), calls=%async_computation.19 | async-start | bytes 5980160 | tf_op jit(solution)/shard_map/reduce_scatter | solution.py:63
  866.5 181.4 %all-gather.33.cloned.1.call-start = ((), (), s32[]{:S(2)}) async-start(), calls=%async_computation.22 | async-start | bytes 2990080 | tf_op jit(solution)/shard_map/all_gather | solution.py:67
  996.3 159.3 %reduce-scatter.23.cloned.1.call-start = ((), (), s32[]{:S(2)}) async-start(), calls=%async_computation.23 | async-start | bytes 2990080 | tf_op jit(solution)/shard_map/reduce_scatter | solution.py:71
  1061.8 8.6 copy-start.21
  1061.8 13.4 slice-start
  1061.8 13.4 slice-start.1
  1109.0 119.3 %all-gather.35.cloned.1.call-start = ((), (), s32[]{:S(2)}) async-start(), calls=%async_computation.24 | async-start | bytes 2990080 | tf_op jit(solution)/shard_map/all_gather | solution.py:67
  1179.2 115.4 %reduce-scatter.25.cloned.1.call-start = ((), (), s32[]{:S(2)}) async-start(), calls=%async_computation.25 | async-start | bytes 2990080 | tf_op jit(solution)/shard_map/reduce_scatter | solution.py:71
  1231.8 8.6 copy-start.74
  1247.9 66.3 %copy-start.16 = (f32[2,577,256]{2,1,0:T(8,128)S(1)}, f32[2,577,256]{2,1,0:T(8,128)}, u32[]{:S(2)}) copy-start(f32[2,577,256]{2,1,0:T(8,128)} %copy-done.15) | copy-start | bytes 3545092
  1247.9 119.7 %all-gather.37.cloned.1.call-start = ((), (), s32[]{:S(2)}) async-start(), calls=%async_computation.26 | async-start | bytes 2990080 | tf_op jit(solution)/shard_map/all_gather | solution.py:67
  1318.5 107.8 %reduce-scatter.33.cloned.1.call-start = ((), (), s32[]{:S(2)}) async-start(), calls=%async_computation.30 | async-start | bytes 4718592 | tf_op jit(solution)/shard_map/reduce_scatter | solution.py:346
  1329.9 144.9 %reduce-scatter.35.cloned.1.call-start = ((), (), s32[]{:S(2)}) async-start(), calls=%async_computation.31 | async-start | bytes 4718592 | tf_op jit(solution)/shard_map/reduce_scatter | solution.py:346
  1341.2 173.2 %reduce-scatter.31.cloned.1.call-start = ((), (), s32[]{:S(2)}) async-start(), calls=%async_computation.29 | async-start | bytes 1179648 | tf_op jit(solution)/shard_map/reduce_scatter | solution.py:346
  1352.6 18.6 %copy-start.38 = (bf16[1,1024,256]{2,1,0:T(8,128)(2,1)S(1)}, bf16[1,1024,256]{2,1,0:T(8,128)(2,1)}, u32[]{:S(2)}) copy-start(bf16[1,1024,256]{2,1,0:T(8,128)(2,1)} %copy-done.37) | copy-start | bytes 1572868
  1380.4 6.8 copy-start.10
  1380.4 6.8 copy-start.57
  1389.8 7.5 copy-start.19
  1397.2 166.7 %reduce-scatter.29.cloned.1.call-start = ((), (), s32[]{:S(2)}) async-start(), calls=%async_computation.28 | async-start | bytes 3538944 | tf_op jit(solution)/shard_map/reduce_scatter | solution.py:346
  1413.2 201.2 %reduce-scatter.27.cloned.1.call-start = ((), (), s32[]{:S(2)}) async-start(), calls=%async_computation.27 | async-start | bytes 2990080 | tf_op jit(solution)/shard_map/reduce_scatter | solution.py:71
  1431.0 43.8 %copy-start.24 = (f32[2,2,128,1024]{3,2,1,0:T(8,128)S(1)}, f32[2,2,128,1024]{3,2,1,0:T(8,128)}, u32[]{:S(2)}) copy-start(f32[2,2,128,1024]{3,2,1,0:T(8,128)} %param.27) | copy-start | bytes 6291460
  1478.0 36.5 %copy-start.41 = (f32[2,2,128,256]{3,2,1,0:T(8,128)S(1)}, f32[2,2,128,256]{3,2,1,0:T(8,128)}, u32[]{:S(2)}) copy-start(f32[2,2,128,256]{3,2,1,0:T(8,128)} %param.25) | copy-start | bytes 1572868
  1478.0 37.4 %copy-start.44 = (f32[2,128,256]{2,1,0:T(8,128)S(1)}, f32[2,128,256]{2,1,0:T(8,128)}, u32[]{:S(2)}) copy-start(f32[2,128,256]{2,1,0:T(8,128)} %param.19) | copy-start | bytes 786436
  1479.4 84.5 %copy-start.29 = (f32[2,2,128,3,256]{4,2,3,1,0:T(8,128)S(1)}, f32[2,2,128,3,256]{4,2,3,1,0:T(8,128)}, u32[]{:S(2)}) copy-start(f32[2,2,128,3,256]{4,2,3,1,0:T(8,128)} %param.24) | copy-start | bytes 4718596
  1515.4 49.6 %copy-start.42 = (f32[2,128,256]{2,1,0:T(8,128)}, f32[2,128,256]{2,1,0:T(8,128)S(1)}, u32[]{:S(2)}) copy-start(f32[2,128,256]{2,1,0:T(8,128)S(1)} %get-tuple-element.131) | copy-start | bytes 786436
  1516.3 48.7 %copy-start.31 = (f32[2,128,3,256]{3,1,2,0:T(8,128)S(1)}, f32[2,128,3,256]{3,1,2,0:T(8,128)}, u32[]{:S(2)}) copy-start(f32[2,128,3,256]{3,1,2,0:T(8,128)} %param.18) | copy-start | bytes 2359300
  1566.5 47.8 %copy-start.6 = (bf16[2,577,256]{2,0,1:T(2,128)(2,1)S(1)}, bf16[2,577,256]{2,0,1:T(2,128)(2,1)}, u32[]{:S(2)}) copy-start(bf16[2,577,256]{2,0,1:T(2,128)(2,1)} %param.15) | copy-start | bytes 1772548
  1566.5 47.8 %copy-start.52 = (f32[2,577]{1,0:T(2,128)S(1)}, f32[2,577]{1,0:T(2,128)}, u32[]{:S(2)}) copy-start(f32[2,577]{1,0:T(2,128)} %copy-done.51) | copy-start | bytes 13852
  1566.5 47.8 %copy-start.54 = (f32[2,577]{1,0:T(2,128)S(1)}, f32[2,577]{1,0:T(2,128)}, u32[]{:S(2)}) copy-start(f32[2,577]{1,0:T(2,128)} %copy-done.53) | copy-start | bytes 13852
  1566.5 47.8 %copy-start.66 = (f32[1,1,256]{2,1,0:T(1,128)S(1)}, f32[1,1,256]{2,1,0:T(1,128)}, u32[]{:S(2)}) copy-start(f32[1,1,256]{2,1,0:T(1,128)} %copy-done.65) | copy-start | bytes 3076
  1566.6 67.0 %copy-start.14 = (f32[2,577,256]{2,1,0:T(8,128)S(1)}, f32[2,577,256]{2,1,0:T(8,128)}, u32[]{:S(2)}) copy-start(f32[2,577,256]{2,1,0:T(8,128)} %copy-done.13) | copy-start | bytes 3545092
  1566.6 67.0 %copy-start.69 = (f32[2]{0:T(128)S(1)}, f32[2]{0:T(128)}, u32[]{:S(2)}) copy-start(f32[2]{0:T(128)} %copy-done.68) | copy-start | bytes 28
  1635.4 24.1 %copy-start.55 = (f32[2,8,256]{2,1,0:T(8,128)S(1)}, f32[2,8,256]{2,1,0:T(8,128)}, u32[]{:S(2)}) copy-start(f32[2,8,256]{2,1,0:T(8,128)} %param.22) | copy-start | bytes 49156
  1635.4 24.1 %copy-start.60 = (f32[2,2,8,256]{3,2,1,0:T(8,128)S(1)}, f32[2,2,8,256]{3,2,1,0:T(8,128)}, u32[]{:S(2)}) copy-start(f32[2,2,8,256]{3,2,1,0:T(8,128)} %param.28) | copy-start | bytes 98308
  1635.4 24.8 %copy-start.62 = (f32[2,1024]{1,0:T(2,128)S(1)}, f32[2,1024]{1,0:T(2,128)}, u32[]{:S(2)}) copy-start(f32[2,1024]{1,0:T(2,128)} %param.23) | copy-start | bytes 24580
  1635.4 24.7 %copy-start.63 = (f32[2,2,1024]{2,1,0:T(2,128)S(1)}, f32[2,2,1024]{2,1,0:T(2,128)}, u32[]{:S(2)}) copy-start(f32[2,2,1024]{2,1,0:T(2,128)} %param.29) | copy-start | bytes 49156
  (46 other events, 124.1 us)
Sparse Core Ops, SparseCore 0:
  32.8 49.2 all-gather.22
  84.6 23.7 all-gather.38
  142.1 86.3 reduce-scatter.12
  249.6 49.4 all-gather.24
  301.4 25.9 all-gather.40
  329.7 27.7 all-gather.42
  369.7 86.3 reduce-scatter.14
  477.1 49.4 all-gather.26
  529.1 23.7 all-gather.44
  588.0 86.3 reduce-scatter.16
  676.5 51.6 all-gather.30
  730.2 49.2 all-gather.28
  781.9 25.9 all-gather.46
  810.3 27.7 all-gather.48
  854.3 48.2 reduce-scatter.20
  904.8 86.0 reduce-scatter.18
  996.4 51.4 all-gather.32
  1109.1 46.4 reduce-scatter.22
  1179.3 48.9 all-gather.34
  1248.0 46.4 reduce-scatter.24
  1318.6 48.9 all-gather.36
  1371.0 49.2 reduce-scatter.32
  1423.7 51.0 reduce-scatter.34
  1478.4 35.9 reduce-scatter.30
  1517.8 46.0 reduce-scatter.28
  1566.0 48.2 reduce-scatter.26
where the time goes:
time: 1680 us; the launch traced here: 1670 us
  waiting for transfers between devices  1080 us (64%)
  blocking collectives  188 us (11%)
  matrix products  160 us (10%)
  local copies, waits for them, and re-layouts  148 us (9%)
  other arithmetic  72.8 us (4%)
    reduce_scatter x4, waiting for transfers between devices, sum_branch(): lax.psum_scatter(partial_rows, 'tensor', scatter_dimension=2, tiled=True)  324 us
    reduce_scatter x4, waiting for transfers between devices, sum_inputs(): lax.psum_scatter(partial_rows.astype(jnp.bfloat16), 'tensor', scatter_dim...  176 us
    all_gather x4, waiting for transfers between devices, share_features(): return lax.all_gather(local_rows, 'tensor', axis=2, tiled=True)  170 us
    all_gather x4, waiting for transfers between devices, share_grads(): return lax.all_gather(local_rows, 'tensor', axis=2, tiled=True)  144 us
    reduce_scatter x4, waiting for transfers between devices, on_device(): lax.psum_scatter(as_sent(stacked), 'dp', scatter_dimension=1, tiled=True)  124 us
    psum x4, blocking collectives, layer_statistics(): lax.psum((jnp.sum(hidden_state, -1), jnp.sum(hidden_state * hidden_state,...  75.1 us
    psum x4, blocking collectives, norm_back(): lax.psum((jnp.sum(d_hat, -1), jnp.sum(d_hat * normed, -1)), 'tensor')  69.8 us
    all_gather x2, waiting for transfers between devices, fetch_weights(): lax.all_gather(pieces[2], 'dp', axis=0, tiled=True)  49.6 us
  transfers between devices with their start and end apart: 26, of which 25 were waited for; matrix products, arithmetic and copies ran while one was open for 10% of the time, Pallas kernels for 0%

commit v1 on v0

v1 whole, which is shorter than its diff:
```python
import jax
import jax.numpy as jnp
from jax import lax
from jax.sharding import PartitionSpec as P

D = 1024
HEADS = 16
LAYERS = 2
STEP = 10


NORM_EPS = 1e-06
ROOT_HALF = 0.7071067811865476
INV_ROOT_TWO_PI = 0.3989422804014327
LEARN_RATE = 0.01
BETA_ONE = 0.9
BETA_TWO = 0.999
ADAM_EPS = 1e-08
WEIGHT_DECAY = 0.05
CONTRACT_LAST = (((1,), (1,)), ((), ()))
CONTRACT_FIRST = (((0,), (0,)), ((), ()))


def gelu_value(preactivation):
    return 0.5 * preactivation * (1.0 + jax.scipy.special.erf(preactivation * ROOT_HALF))


def gelu_slope(preactivation):
    return (
        0.5 * (1.0 + jax.scipy.special.erf(preactivation * ROOT_HALF))
        + preactivation * jnp.exp(-0.5 * preactivation * preactivation) * INV_ROOT_TWO_PI
    )


def norm_full(hidden_low, gain_full, shift_full):
    wide = hidden_low.astype(jnp.float32)
    mean_row = jnp.mean(wide, -1, keepdims=True)
    spread = jnp.mean(wide * wide, -1, keepdims=True) - mean_row * mean_row
    inv_std = lax.rsqrt(spread + NORM_EPS)
    normalized = ((wide - mean_row) * inv_std * gain_full + shift_full).astype(jnp.bfloat16)
    return normalized, mean_row, inv_std


def share_features(local_rows):
    return lax.all_gather(local_rows, "tensor", axis=1, tiled=True)


def sum_branch(partial_rows):
    return lax.psum_scatter(
        partial_rows.astype(jnp.bfloat16), "tensor", scatter_dimension=1, tiled=True
    ).astype(jnp.float32)


def sum_with_totals(partial_rows, hidden_low, mean_row, inv_std, gain_full):
    rows, width = partial_rows.shape
    parts = lax.axis_size("tensor")
    chunk = width // parts
    d_hat = partial_rows * gain_full
    normed = (hidden_low.astype(jnp.float32) - mean_row) * inv_std
    sums = jnp.concatenate([jnp.sum(d_hat, -1), jnp.sum(d_hat * normed, -1)])
    extra = -(-2 * rows // (16 * chunk)) * 16
    sums = jnp.pad(sums, (0, extra * chunk - 2 * rows)).reshape(extra, chunk)
    operand = jnp.concatenate(
        [
            partial_rows.astype(jnp.bfloat16),
            jnp.tile(sums.astype(jnp.bfloat16), (1, parts)),
        ]
    )
    summed = lax.psum_scatter(operand, "tensor", scatter_dimension=1, tiled=True).astype(
        jnp.float32
    )
    flat = summed[rows:].reshape(-1)
    return summed[:rows], flat[:rows, None], flat[rows : 2 * rows, None]


def norm_back(d_normed, total_plain, total_normed, normed, inv_std, gain, carried):
    d_hat = d_normed * gain
    grad_in = carried + inv_std * (d_hat - total_plain / D - normed * total_normed / D)
    return (grad_in, jnp.sum(d_normed * normed, 0), jnp.sum(d_normed, 0))


def swap_dp(value, bit):
    count = lax.axis_size("dp")
    return lax.ppermute(value, "dp", [(i, i ^ bit) for i in range(count)])


def dp_bits():
    count = lax.axis_size("dp")
    return [1 << i for i in range(count.bit_length() - 1)]


def gather_rows(shard):
    count = lax.axis_size("dp")
    me = lax.axis_index("dp")
    pieces = {0: shard}
    for bit in reversed(dp_bits()):
        for offset in sorted(pieces):
            pieces[offset | bit] = swap_dp(pieces[offset], bit)
    whole = jnp.zeros((count,) + shard.shape, shard.dtype)
    for offset in range(count):
        whole = lax.dynamic_update_index_in_dim(whole, pieces[offset], me ^ offset, 0)
    return whole.reshape((count * shard.shape[0],) + shard.shape[1:])


def scatter_rows(parts):
    count = lax.axis_size("dp")
    me = lax.axis_index("dp")
    share = parts[0].shape[0] // count
    pieces = {}
    for offset in range(count):
        start = (me ^ offset) * share
        pieces[offset] = jnp.concatenate(
            [lax.dynamic_slice_in_dim(part, start, share, 0) for part in parts], axis=1
        )
    for bit in dp_bits():
        kept = {}
        for offset in sorted(pieces):
            if not offset & bit:
                arrived = swap_dp(pieces[offset | bit], bit)
                kept[offset] = (
                    pieces[offset].astype(jnp.float32) + arrived.astype(jnp.float32)
                )
        if len(kept) > 1:
            kept = {k: v.astype(jnp.bfloat16) for k, v in kept.items()}
        pieces = kept
    return pieces[0]


def sum_dp(value):
    for bit in dp_bits():
        value = value + swap_dp(value, bit)
    return value


def fetch_weights(w_qkv, w_out, w_fc1, w_fc2, layer_number):
    rows = w_qkv.shape[1]
    chunk = w_out.shape[2]
    attn = jnp.concatenate(
        [w_qkv[layer_number].reshape(rows, 3 * chunk), w_out[layer_number]], axis=1
    ).astype(jnp.bfloat16)
    return (
        gather_rows(attn),
        gather_rows(w_fc1[layer_number].astype(jnp.bfloat16)),
        gather_rows(w_fc2[layer_number].astype(jnp.bfloat16)),
    )


def attend_forward(query_h, key_h, value_h, attn_scale):
    scores = (
        jnp.einsum("bqhd,bkhd->bhqk", query_h, key_h, preferred_element_type=jnp.float32)
        * attn_scale
    )
    top_score = jnp.max(scores, -1, keepdims=True)
    logged_total = top_score + jnp.log(jnp.sum(jnp.exp(scores - top_score), -1, keepdims=True))
    probs = jnp.exp(scores - logged_total).astype(jnp.bfloat16)
    attention_result = jnp.einsum(
        "bhqk,bkhd->bqhd", probs, value_h, preferred_element_type=jnp.float32
    ).astype(jnp.bfloat16)
    return (attention_result, logged_total)


def attend_backward(query_h, key_h, value_h, attention_result, d_att, logged_total, attn_scale):
    scores = (
        jnp.einsum("bqhd,bkhd->bhqk", query_h, key_h, preferred_element_type=jnp.float32)
        * attn_scale
    )
    probs = jnp.exp(scores - logged_total)
    probs_low = probs.astype(jnp.bfloat16)
    d_value = jnp.einsum("bhqk,bqhd->bkhd", probs_low, d_att, preferred_element_type=jnp.float32)
    d_probs = jnp.einsum("bqhd,bkhd->bhqk", d_att, value_h, preferred_element_type=jnp.float32)
    delta = jnp.sum(d_att.astype(jnp.float32) * attention_result.astype(jnp.float32), -1)
    d_scores = (probs * (d_probs - jnp.swapaxes(delta, 1, 2)[..., None]) * attn_scale).astype(
        jnp.bfloat16
    )
    d_query = jnp.einsum("bhqk,bkhd->bqhd", d_scores, key_h, preferred_element_type=jnp.float32)
    d_key = jnp.einsum("bhqk,bqhd->bkhd", d_scores, query_h, preferred_element_type=jnp.float32)
    return (d_query, d_key, d_value)


def adam_update(param, running_gradient, moments, decay):
    first = BETA_ONE * moments[0] + (1.0 - BETA_ONE) * running_gradient
    second = BETA_TWO * moments[1] + (1.0 - BETA_TWO) * running_gradient * running_gradient
    fix_one = 1.0 - BETA_ONE**STEP
    fix_two = 1.0 - BETA_TWO**STEP
    update = first / fix_one / (jnp.sqrt(second / fix_two) + ADAM_EPS) + decay * param
    return (param - LEARN_RATE * update, jnp.stack([first, second]))


def on_device(
    tokens,
    cotangent,
    image_counts,
    w_qkv,
    w_out,
    w_fc1,
    w_fc2,
    vec_small,
    fc1_bias,
    mom_qkv,
    mom_out,
    mom_fc1,
    mom_fc2,
    mom_vec,
    mom_bias,
):
    slot_count, seq_len, feat_width = tokens.shape
    tok_rows = slot_count * seq_len
    heads_here = HEADS // lax.axis_size("tensor")
    head_dim = feat_width // heads_here
    attn_scale = head_dim ** (-0.5)
    row_number = lax.broadcasted_iota(jnp.int32, (tok_rows, 1), 0)
    row_live = jnp.where((row_number < seq_len) | (image_counts[0] == 2), 1.0, 0.0)
    vec_full = lax.all_gather(vec_small, "tensor", axis=2, tiled=True)

    def to_heads(matrix):
        return matrix.reshape(slot_count, seq_len, heads_here, head_dim)

    hidden_low = tokens.reshape(tok_rows, feat_width)
    hidden_state = hidden_low.astype(jnp.float32)
    fetched = [fetch_weights(w_qkv, w_out, w_fc1, w_fc2, n) for n in range(LAYERS)]
    qkv_width = 3 * feat_width
    saved_tensors = []
    for layer_number in range(LAYERS):
        attn_weight, first_weight, second_weight = fetched[layer_number]
        qkv_weight = attn_weight[:, :qkv_width]
        out_weight = attn_weight[:, qkv_width:]
        vector_rows = vec_small[layer_number]
        full_rows = vec_full[layer_number]
        first_low = share_features(hidden_state.astype(jnp.bfloat16))
        first_normalized, first_mean, first_inv = norm_full(first_low, full_rows[0], full_rows[1])
        first_hat = (hidden_state - first_mean) * first_inv
        proj_out = jnp.dot(first_normalized, qkv_weight, preferred_element_type=jnp.float32)
        query_rows = (proj_out[:, :feat_width] + vector_rows[2]).astype(jnp.bfloat16)
        key_rows = proj_out[:, feat_width : 2 * feat_width].astype(jnp.bfloat16)
        value_rows = (proj_out[:, 2 * feat_width :] + vector_rows[3]).astype(jnp.bfloat16)
        attention_result, logged_total = attend_forward(
            to_heads(query_rows), to_heads(key_rows), to_heads(value_rows), attn_scale
        )
        attention_result = attention_result.reshape(tok_rows, feat_width)
        if layer_number == LAYERS - 1:
            last_gradient = cotangent.reshape(tok_rows, feat_width) * row_live
            last_low, first_normalized = lax.optimization_barrier(
                (last_gradient.astype(jnp.bfloat16), first_normalized)
            )
            last_full, attention_result = lax.optimization_barrier(
                (share_features(last_low), attention_result)
            )
        attn_branch = sum_branch(
            lax.dot_general(
                attention_result, out_weight, CONTRACT_LAST, preferred_element_type=jnp.float32
            )
        )
        middle_state = hidden_state + attn_branch + vector_rows[4]
        second_low = share_features(middle_state.astype(jnp.bfloat16))
        second_normalized, second_mean, second_inv = norm_full(
            second_low, full_rows[5], full_rows[6]
        )
        second_hat = (middle_state - second_mean) * second_inv
        preactivation = (
            jnp.dot(second_normalized, first_weight, preferred_element_type=jnp.float32)
            + fc1_bias[layer_number]
        )
        activation_narrow = gelu_value(preactivation).astype(jnp.bfloat16)
        branch_two = lax.dot_general(
            activation_narrow, second_weight, CONTRACT_LAST, preferred_element_type=jnp.float32
        )
        saved_tensors.append(
            (
                first_low,
                first_mean,
                first_inv,
                first_hat,
                first_normalized,
                query_rows,
                key_rows,
                value_rows,
                attention_result,
                logged_total,
                second_low,
                second_mean,
                second_inv,
                second_hat,
                second_normalized,
                preactivation,
                activation_narrow,
            )
        )
        if layer_number < LAYERS - 1:
            hidden_state = middle_state + sum_branch(branch_two) + vector_rows[7]
    running_gradient = last_gradient
    big_grads = [None] * LAYERS
    vec_grads = [None] * LAYERS
    bias_grads = [None] * LAYERS
    for layer_number in reversed(range(LAYERS)):
        attn_weight, first_weight, second_weight = fetched[layer_number]
        qkv_weight = attn_weight[:, :qkv_width]
        out_weight = attn_weight[:, qkv_width:]
        vector_rows = vec_small[layer_number]
        full_rows = vec_full[layer_number]
        (
            first_low,
            first_mean,
            first_inv,
            first_hat,
            first_normalized,
            query_rows,
            key_rows,
            value_rows,
            attention_result,
            logged_total,
            second_low,
            second_mean,
            second_inv,
            second_hat,
            second_normalized,
            preactivation,
            activation_narrow,
        ) = saved_tensors[layer_number]
        full_grad = last_full
        if layer_number < LAYERS - 1:
            full_grad = share_features(running_gradient.astype(jnp.bfloat16))
        g_bias_two = jnp.sum(running_gradient, 0)
        d_pre = jnp.dot(full_grad, second_weight, preferred_element_type=jnp.float32) * gelu_slope(
            preactivation
        )
        d_pre_low = d_pre.astype(jnp.bfloat16)
        g_fc1_bias = jnp.sum(d_pre, 0)
        second_grad, plain_total, normed_total = sum_with_totals(
            lax.dot_general(
                d_pre_low, first_weight, CONTRACT_LAST, preferred_element_type=jnp.float32
            ),
            second_low,
            second_mean,
            second_inv,
            full_rows[5],
        )
        g_fc2 = lax.dot_general(
            full_grad, activation_narrow, CONTRACT_FIRST, preferred_element_type=jnp.float32
        ).astype(jnp.bfloat16)
        g_fc1 = lax.dot_general(
            second_normalized, d_pre_low, CONTRACT_FIRST, preferred_element_type=jnp.float32
        ).astype(jnp.bfloat16)
        s_fc1 = scatter_rows([g_fc1])
        s_fc2 = scatter_rows([g_fc2])
        middle_gradient, second_gain_gradient, second_shift_gradient = norm_back(
            second_grad,
            plain_total,
            normed_total,
            second_hat,
            second_inv,
            vector_rows[5],
            running_gradient,
        )
        full_mid = share_features(middle_gradient.astype(jnp.bfloat16))
        g_out = lax.dot_general(
            full_mid, attention_result, CONTRACT_FIRST, preferred_element_type=jnp.float32
        ).astype(jnp.bfloat16)
        g_bias_out = jnp.sum(middle_gradient, 0)
        d_att = jnp.dot(full_mid, out_weight, preferred_element_type=jnp.float32).astype(
            jnp.bfloat16
        )
        d_query, d_key, d_value = attend_backward(
            to_heads(query_rows),
            to_heads(key_rows),
            to_heads(value_rows),
            to_heads(attention_result),
            to_heads(d_att),
            logged_total,
            attn_scale,
        )
        if layer_number == LAYERS - 1:
            branch_low, full_mid = lax.optimization_barrier(
                (branch_two.astype(jnp.bfloat16), full_mid)
            )
            last_branch, d_query, d_key, d_value = lax.optimization_barrier(
                (sum_branch(branch_low), d_query, d_key, d_value)
            )
            output = ((middle_state + last_branch + vector_rows[7]) * row_live).reshape(
                tokens.shape
            )
        d_query = d_query.reshape(tok_rows, feat_width)
        d_key = d_key.reshape(tok_rows, feat_width)
        d_value = d_value.reshape(tok_rows, feat_width)
        d_proj = jnp.concatenate(
            [d_query.astype(jnp.bfloat16), d_key.astype(jnp.bfloat16), d_value.astype(jnp.bfloat16)],
            axis=1,
        )
        first_grad, plain_total, normed_total = sum_with_totals(
            lax.dot_general(
                d_proj, qkv_weight, CONTRACT_LAST, preferred_element_type=jnp.float32
            ),
            first_low,
            first_mean,
            first_inv,
            full_rows[0],
        )
        g_qkv = lax.dot_general(
            first_normalized, d_proj, CONTRACT_FIRST, preferred_element_type=jnp.float32
        ).astype(jnp.bfloat16)
        s_attn = scatter_rows([g_qkv, g_out])
        running_gradient, first_gain_gradient, first_shift_gradient = norm_back(
            first_grad,
            plain_total,
            normed_total,
            first_hat,
            first_inv,
            vector_rows[0],
            middle_gradient,
        )
        vec_grads[layer_number] = jnp.stack(
            [
                first_gain_gradient,
                first_shift_gradient,
                jnp.sum(d_query, 0),
                jnp.sum(d_value, 0),
                g_bias_out,
                second_gain_gradient,
                second_shift_gradient,
                g_bias_two,
            ]
        )
        bias_grads[layer_number] = g_fc1_bias
        big_grads[layer_number] = (
            s_attn[:, :qkv_width].reshape(-1, 3, feat_width),
            s_attn[:, qkv_width:],
            s_fc1,
            s_fc2,
        )
    input_grad = (running_gradient * row_live).reshape(tokens.shape)
    stacked = tuple(jnp.stack([entry[which] for entry in big_grads]) for which in range(4))
    vec_rows = vec_small.shape[0] * vec_small.shape[1]
    small = sum_dp(
        jnp.concatenate(
            [
                jnp.stack(vec_grads).reshape(vec_rows, feat_width),
                jnp.stack(bias_grads).reshape(-1, feat_width),
            ]
        )
    )
    small_sums = (small[:vec_rows].reshape(vec_small.shape), small[vec_rows:].reshape(fc1_bias.shape))
    grad_totals = (stacked[0], stacked[1], stacked[2], stacked[3], small_sums[0], small_sums[1])
    params = (w_qkv, w_out, w_fc1, w_fc2, vec_small, fc1_bias)
    moments = (mom_qkv, mom_out, mom_fc1, mom_fc2, mom_vec, mom_bias)
    decays = (WEIGHT_DECAY, WEIGHT_DECAY, WEIGHT_DECAY, WEIGHT_DECAY, 0.0, 0.0)
    results = [
        adam_update(param, grad_total, moment, decay)
        for param, grad_total, moment, decay in zip(params, grad_totals, moments, decays)
    ]
    return (
        output,
        input_grad,
        grad_totals[0],
        grad_totals[1],
        grad_totals[2],
        grad_totals[3],
        grad_totals[4],
        grad_totals[5],
        results[0][0],
        results[1][0],
        results[2][0],
        results[3][0],
        results[4][0],
        results[5][0],
        results[0][1],
        results[1][1],
        results[2][1],
        results[3][1],
        results[4][1],
        results[5][1],
    )


def solution(mesh):
    return jax.shard_map(
        on_device,
        mesh=mesh,
        in_specs=(
            P("dp", None, "tensor"),
            P("dp", None, "tensor"),
            P("dp"),
            P(None, "dp", None, "tensor"),
            P(None, "dp", "tensor"),
            P(None, "dp", "tensor"),
            P(None, "dp", "tensor"),
            P(None, None, "tensor"),
            P(None, "tensor"),
            P(None, None, "dp", None, "tensor"),
            P(None, None, "dp", "tensor"),
            P(None, None, "dp", "tensor"),
            P(None, None, "dp", "tensor"),
            P(None, None, None, "tensor"),
            P(None, None, "tensor"),
        ),
        out_specs=(
            P("dp", None, "tensor"),
            P("dp", None, "tensor"),
            P(None, "dp", None, "tensor"),
            P(None, "dp", "tensor"),
            P(None, "dp", "tensor"),
            P(None, "dp", "tensor"),
            P(None, None, "tensor"),
            P(None, "tensor"),
            P(None, "dp", None, "tensor"),
            P(None, "dp", "tensor"),
            P(None, "dp", "tensor"),
            P(None, "dp", "tensor"),
            P(None, None, "tensor"),
            P(None, "tensor"),
            P(None, None, "dp", None, "tensor"),
            P(None, None, "dp", "tensor"),
            P(None, None, "dp", "tensor"),
            P(None, None, "dp", "tensor"),
            P(None, None, None, "tensor"),
            P(None, None, "tensor"),
        ),
        check_vma=False,
    )
```

time: 1680 us -> 1020 us (0.61)
  waiting for transfers between devices: 1080 us -> 490 us
  blocking collectives: 188 us -> 13.9 us
  starting transfers between devices: 2.37 us -> 57.9 us
  other arithmetic: 72.8 us -> 116 us
    reduce_scatter x12 -> x8, waiting for transfers between devices: 624 us -> 252 us  [the longest x4 146 us: sum_branch(): lax.psum_scatter(partial_rows.astype(jnp.bfloat16), 'tensor', scatter_dim...]
    all_gather x14 -> x8, waiting for transfers between devices: 455 us -> 188 us  [share_features(): return lax.all_gather(local_rows, 'tensor', axis=1, tiled=True)]
    psum x9 -> x0, blocking collectives: 167 us -> none  [the longest x4 75.1 us: layer_statistics(): lax.psum((jnp.sum(hidden_state, -1), jnp.sum(hidden_state * hidden_state,...]
    ppermute x0 -> x87, starting transfers between devices: none -> 56.5 us  [swap_dp(): return lax.ppermute(value, 'dp', [(i, i ^ bit) for i in range(count)])]
    ppermute x0 -> x87, waiting for transfers between devices: none -> 49.4 us  [swap_dp(): return lax.ppermute(value, 'dp', [(i, i ^ bit) for i in range(count)])]
    dynamic_update_slice x0 -> x45, local copies, waits for them, and re-layouts: none -> 34.7 us  [gather_rows(): lax.dynamic_update_index_in_dim(whole, pieces[offset], me ^ offset, 0)]
    reshape x10 -> x7, local copies, waits for them, and re-layouts: 38.2 us -> 3.99 us  [the longest x1 1.47 us: on_device(): last_gradient = cotangent.reshape(tok_rows, feat_width) * row_live]
    convert_element_type x8 -> x29, other arithmetic: 12 us -> 36.2 us  [the longest x14 14.9 us: scatter_rows(): kept = {k: v.astype(jnp.bfloat16) for k, v in kept.items()}]
  transfers between devices with their start and end apart: 26 -> 103, of which waited for: 25 -> 32; matrix products, arithmetic and copies ran while one was open for 10% -> 25% of each run, Pallas kernels for 0% -> 0%
where the time goes in v1:
time: 1020 us; the launch traced here: 1010 us
  waiting for transfers between devices  490 us (48%)
  local copies, waits for them, and re-layouts  160 us (16%)
  matrix products  156 us (15%)
  other arithmetic  116 us (11%)
  starting transfers between devices  57.9 us (6%)
  between operations  17.3 us (2%)
  blocking collectives  13.9 us (1%)
    all_gather x8, waiting for transfers between devices, share_features(): return lax.all_gather(local_rows, 'tensor', axis=1, tiled=True)  188 us
    reduce_scatter x4, waiting for transfers between devices, sum_branch(): lax.psum_scatter(partial_rows.astype(jnp.bfloat16), 'tensor', scatter_dim...  146 us
    reduce_scatter x4, waiting for transfers between devices, sum_with_totals(): lax.psum_scatter(operand, 'tensor', scatter_dimension=1, tiled=True)  105 us
    ppermute x87, starting transfers between devices, swap_dp(): return lax.ppermute(value, 'dp', [(i, i ^ bit) for i in range(count)])  56.5 us
    ppermute x87, waiting for transfers between devices, swap_dp(): return lax.ppermute(value, 'dp', [(i, i ^ bit) for i in range(count)])  49.4 us
    dynamic_update_slice x45, local copies, waits for them, and re-layouts, gather_rows(): lax.dynamic_update_index_in_dim(whole, pieces[offset], me ^ offset, 0)  34.7 us
    unnamed x332, local copies, waits for them, and re-layouts  33.2 us
    reshape x15, local copies, waits for them, and re-layouts, to_heads(): return matrix.reshape(slot_count, seq_len, heads_here, head_dim)  25 us
  transfers between devices with their start and end apart: 103, of which 32 were waited for; matrix products, arithmetic and copies ran while one was open for 25% of the time, Pallas kernels for 0%

profile of v1, /device:TPU:0, one launch (start us, length us, event | category | flops | bytes accessed | tf_op | source)
XLA Modules:
  0.0 1010.3 jit_solution(7716534504172338927)
XLA Ops:
  9.9 3.1 collective-permute-start.3
  14.5 13.9 %all_gather.28 = f32[2,8,1024]{2,1,0:T(8,128)S(1)} all-gather(f32[2,8,256]{2,1,0:T(8,128)S(1)} %copy-done.90), channel_id=1, replica_groups=mesh['dp'=8,'tensor'=4] {'tensor'}, dimensions={2}, use_global_device_ids=true | all-gather | bytes 81920 | tf_op jit(solution)/shard_map/all_gather | solution.py:213
  33.7 2.7 collective-permute-done.5
  38.9 25.3 %all-gather.9.cloned.1.call-done = bf16[1154,1024]{1,0:T(8,128)(2,1)} async-done(((bf16[1154,256]{1,0:T(8,128)(2,1)}), bf16[1154,1024]{1,0:T(8,128)(2,1)}) %all-gather.9.cloned.1.call-update) | async-done | bytes 2363408 | tf_op jit(solution)/shard_map/all_gather | solution.py:45
  64.2 2.6 convert_reduce_fusion.3
  66.9 2.6 fusion.44
  87.2 3.6 convolution_convert_fusion.3
  99.8 37.2 %reduce-scatter.9.cloned.1.call-done = bf16[1154,256]{1,0:T(8,128)(2,1)} async-done(((bf16[1154,1024]{1,0:T(8,128)(2,1)}), bf16[1154,256]{1,0:T(8,128)(2,1)}) %reduce-scatter.9.cloned.1.call-update) | async-done | bytes 590864 | tf_op jit(solution)/shard_map/reduce_scatter | solution.py:49
  145.4 3.7 collective-permute-done.19
  149.7 4.6 collective-permute-done.12
  161.5 28.0 %all-gather.11.cloned.1.call-done = bf16[1154,1024]{1,0:T(8,128)(2,1)} async-done(((bf16[1154,256]{1,0:T(8,128)(2,1)}), bf16[1154,1024]{1,0:T(8,128)(2,1)}) %all-gather.11.cloned.1.call-update) | async-done | bytes 2363408 | tf_op jit(solution)/shard_map/all_gather | solution.py:45
  192.1 7.0 multiply_convert_fusion.3
  200.5 5.6 convolution_convert_fusion.2
  206.2 46.5 %reduce-scatter.11.cloned.1.call-done = bf16[1154,256]{1,0:T(8,128)(2,1)} async-done(((bf16[1154,1024]{1,0:T(8,128)(2,1)}), bf16[1154,256]{1,0:T(8,128)(2,1)}) %reduce-scatter.11.cloned.1.call-update) | async-done | bytes 590864 | tf_op jit(solution)/shard_map/reduce_scatter | solution.py:49
  269.8 5.3 collective-permute-done.26
  277.3 28.0 %all-gather.13.cloned.1.call-done = bf16[1154,1024]{1,0:T(8,128)(2,1)} async-done(((bf16[1154,256]{1,0:T(8,128)(2,1)}), bf16[1154,1024]{1,0:T(8,128)(2,1)}) %all-gather.13.cloned.1.call-update) | async-done | bytes 2363408 | tf_op jit(solution)/shard_map/all_gather | solution.py:45
  312.5 4.2 fusion.40
  322.1 3.2 reshape.894
  327.7 2.9 reshape.892
  333.0 3.2 multiply_reduce_fusion
  347.0 13.1 %all-gather.15.cloned.1.call-done = bf16[1154,1024]{1,0:T(8,128)(2,1)} async-done(((bf16[1154,256]{1,0:T(8,128)(2,1)}), bf16[1154,1024]{1,0:T(8,128)(2,1)}) %all-gather.15.cloned.1.call-update) | async-done | bytes 2363408 | tf_op jit(solution)/shard_map/all_gather | solution.py:45
  360.1 3.3 convolution_convert_fusion.1
  371.5 38.5 %reduce-scatter.13.cloned.1.call-done = bf16[1154,256]{1,0:T(8,128)(2,1)} async-done(((bf16[1154,1024]{1,0:T(8,128)(2,1)}), bf16[1154,256]{1,0:T(8,128)(2,1)}) %reduce-scatter.13.cloned.1.call-update) | async-done | bytes 590864 | tf_op jit(solution)/shard_map/reduce_scatter | solution.py:49
  427.9 3.1 collective-permute-done.33
  439.6 22.7 %all-gather.17.cloned.1.call-done = bf16[1154,1024]{1,0:T(8,128)(2,1)} async-done(((bf16[1154,256]{1,0:T(8,128)(2,1)}), bf16[1154,1024]{1,0:T(8,128)(2,1)}) %all-gather.17.cloned.1.call-update) | async-done | bytes 2363408 | tf_op jit(solution)/shard_map/all_gather | solution.py:45
  465.0 6.8 multiply_convert_fusion.2
  471.8 6.1 fusion.186
  477.9 7.0 multiply_reduce_fusion.5
  485.0 3.4 pad_maximum_fusion
  488.5 47.2 %reduce-scatter.15.cloned.1.call-done = bf16[1170,256]{1,0:T(8,128)(2,1)} async-done(((bf16[1170,1024]{1,0:T(8,128)(2,1)}), bf16[1170,256]{1,0:T(8,128)(2,1)}) %reduce-scatter.15.cloned.1.call-update) | async-done | bytes 599056 | tf_op jit(solution)/shard_map/reduce_scatter | solution.py:69
  540.4 6.4 convolution_convert_fusion
  546.8 43.8 %all-gather.19.cloned.1.call-done = bf16[1154,1024]{1,0:T(8,128)(2,1)} async-done(((bf16[1154,256]{1,0:T(8,128)(2,1)}), bf16[1154,1024]{1,0:T(8,128)(2,1)}) %all-gather.19.cloned.1.call-update) | async-done | bytes 2363408 | tf_op jit(solution)/shard_map/all_gather | solution.py:45
  599.5 8.3 multiply_convert_fusion.1
  607.8 2.7 convolution_bitcast_fusion.3
  615.1 24.2 %reduce-scatter.17.cloned.1.call-done = bf16[1154,256]{1,0:T(8,128)(2,1)} async-done(((bf16[1154,1024]{1,0:T(8,128)(2,1)}), bf16[1154,256]{1,0:T(8,128)(2,1)}) %reduce-scatter.17.cloned.1.call-update) | async-done | bytes 590864 | tf_op jit(solution)/shard_map/reduce_scatter | solution.py:49
  645.3 3.0 fusion.179
  654.4 7.1 multiply_reduce_fusion.4
  661.6 3.3 pad_maximum_fusion.1
  665.0 48.4 %reduce-scatter.19.cloned.1.call-done = bf16[1170,256]{1,0:T(8,128)(2,1)} async-done(((bf16[1170,1024]{1,0:T(8,128)(2,1)}), bf16[1170,256]{1,0:T(8,128)(2,1)}) %reduce-scatter.19.cloned.1.call-update) | async-done | bytes 599056 | tf_op jit(solution)/shard_map/reduce_scatter | solution.py:69
  714.7 3.8 slice_reduce_fusion.2
  722.3 5.9 convolution_convert_fusion.8
  728.9 3.3 convolution_convert_fusion.6
  747.4 22.3 %all-gather.21.cloned.1.call-done = bf16[1154,1024]{1,0:T(8,128)(2,1)} async-done(((bf16[1154,256]{1,0:T(8,128)(2,1)}), bf16[1154,1024]{1,0:T(8,128)(2,1)}) %all-gather.21.cloned.1.call-update) | async-done | bytes 2363408 | tf_op jit(solution)/shard_map/all_gather | solution.py:45
  769.8 7.7 fusion.187
  777.5 7.0 multiply_reduce_fusion.3
  784.7 3.3 pad_maximum_fusion.2
  805.1 6.7 collective-permute-done.54
  817.0 3.2 collective-permute-done.55
  821.4 5.8 convolution_convert_fusion.9
  830.0 5.3 reduce-scatter.21.cloned.1.call-done
  840.3 5.3 convolution_convert_fusion.7
  864.9 6.6 collective-permute-done.75
  885.4 5.0 all-gather.23.cloned.1.call-done
  896.9 7.5 fusion.177
  904.4 6.3 multiply_convert_fusion
  915.8 2.6 copy.297
  920.5 2.6 copy.291
  923.1 2.8 convert_element_type.749
  927.7 7.1 multiply_reduce_fusion.2
  935.0 3.4 pad_maximum_fusion.3
  939.7 3.9 multiply_subtract_fusion.1
  954.1 6.8 collective-permute-done.47
  981.2 4.5 reduce-scatter.23.cloned.1.call-done
  992.2 2.7 pad_maximum_fusion.6
  (785 shorter events, 320.3 us)
Async XLA Ops:
  7.2 57.0 %all-gather.9.cloned.1.call-start = ((), (), s32[]{:S(2)}) async-start(), calls=%async_computation.8 | async-start | bytes 2969600 | tf_op jit(solution)/shard_map/all_gather | solution.py:45
  9.5 127.5 %reduce-scatter.9.cloned.1.call-start = ((), (), s32[]{:S(2)}) async-start(), calls=%async_computation.9 | async-start | bytes 2969600 | tf_op jit(solution)/shard_map/reduce_scatter | solution.py:49
  9.9 19.9 %collective-permute-start.3 = (bf16[128,1024]{0,1:T(8,128)(2,1)S(1)}, bf16[128,1024]{0,1:T(8,128)(2,1)S(1)}, u32[]{:S(2)}, u32[]{:S(2)}) collective-permute-start(bf16[128,1024]{0,1:T(8,128)(2,1)S(1)} %pad_maximum_fusion.15), channel_id=1, source_target_pairs={{0,16},{4,20},{8,24},{12,28},{16,0},{20,4},{24,8},{28,12},{1,17},{... | collective-permute-start | bytes 786440 | tf_op jit(solution)/shard_map/ppermute | solution.py:84
  13.0 17.3 %collective-permute-start.1 = (bf16[128,1024]{0,1:T(8,128)(2,1)S(1)}, bf16[128,1024]{0,1:T(8,128)(2,1)S(1)}, u32[]{:S(2)}, u32[]{:S(2)}) collective-permute-start(bf16[128,1024]{0,1:T(8,128)(2,1)S(1)} %pad_maximum_fusion.15), channel_id=1, source_target_pairs={{0,8},{4,12},{8,0},{12,4},{16,24},{20,28},{24,16},{28,20},{1,9},{5... | collective-permute-start | bytes 786440 | tf_op jit(solution)/shard_map/ppermute | solution.py:84
  14.5 16.3 %collective-permute-start = (bf16[128,1024]{0,1:T(8,128)(2,1)S(1)}, bf16[128,1024]{0,1:T(8,128)(2,1)}, u32[]{:S(2)}, u32[]{:S(2)}) collective-permute-start(bf16[128,1024]{0,1:T(8,128)(2,1)S(1)} %pad_maximum_fusion.15), channel_id=1, source_target_pairs={{0,4},{4,0},{8,12},{12,8},{16,20},{20,16},{24,28},{28,24},{1,5},{5... | collective-permute-start | bytes 786440 | tf_op jit(solution)/shard_map/ppermute | solution.py:84
  90.7 98.7 %all-gather.11.cloned.1.call-start = ((), (), s32[]{:S(2)}) async-start(), calls=%async_computation.10 | async-start | bytes 2969600 | tf_op jit(solution)/shard_map/all_gather | solution.py:45
  93.2 46.7 %collective-permute-start.17 = (bf16[128,1024]{1,0:T(8,128)(2,1)S(1)}, bf16[128,1024]{1,0:T(8,128)(2,1)S(1)}, u32[]{:S(2)}, u32[]{:S(2)}) collective-permute-start(bf16[128,1024]{1,0:T(8,128)(2,1)S(1)} %get-tuple-element.237), channel_id=1, source_target_pairs={{0,16},{4,20},{8,24},{12,28},{16,0},{20,4},{24,8},{28,12},{1,17},{... | collective-permute-start | bytes 786440 | tf_op jit(solution)/shard_map/ppermute | solution.py:84
  94.4 47.8 %collective-permute-start.15 = (bf16[128,1024]{1,0:T(8,128)(2,1)S(1)}, bf16[128,1024]{1,0:T(8,128)(2,1)S(1)}, u32[]{:S(2)}, u32[]{:S(2)}) collective-permute-start(bf16[128,1024]{1,0:T(8,128)(2,1)S(1)} %get-tuple-element.237), channel_id=1, source_target_pairs={{0,8},{4,12},{8,0},{12,4},{16,24},{20,28},{24,16},{28,20},{1,9},{5... | collective-permute-start | bytes 786440 | tf_op jit(solution)/shard_map/ppermute | solution.py:84
  95.8 44.1 %collective-permute-start.14 = (bf16[128,1024]{1,0:T(8,128)(2,1)S(1)}, bf16[128,1024]{1,0:T(8,128)(2,1)S(1)}, u32[]{:S(2)}, u32[]{:S(2)}) collective-permute-start(bf16[128,1024]{1,0:T(8,128)(2,1)S(1)} %get-tuple-element.237), channel_id=1, source_target_pairs={{0,4},{4,0},{8,12},{12,8},{16,20},{20,16},{24,28},{28,24},{1,5},{5... | collective-permute-start | bytes 786440 | tf_op jit(solution)/shard_map/ppermute | solution.py:84
  98.3 44.8 %collective-permute-start.10 = (bf16[128,1024]{1,0:T(8,128)(2,1)S(1)}, bf16[128,1024]{1,0:T(8,128)(2,1)S(1)}, u32[]{:S(2)}, u32[]{:S(2)}) collective-permute-start(bf16[128,1024]{1,0:T(8,128)(2,1)S(1)} %get-tuple-element.239), channel_id=1, source_target_pairs={{0,16},{4,20},{8,24},{12,28},{16,0},{20,4},{24,8},{28,12},{1,17},{... | collective-permute-start | bytes 786440 | tf_op jit(solution)/shard_map/ppermute | solution.py:84
  98.9 45.8 %collective-permute-start.8 = (bf16[128,1024]{1,0:T(8,128)(2,1)S(1)}, bf16[128,1024]{1,0:T(8,128)(2,1)S(1)}, u32[]{:S(2)}, u32[]{:S(2)}) collective-permute-start(bf16[128,1024]{1,0:T(8,128)(2,1)S(1)} %get-tuple-element.239), channel_id=1, source_target_pairs={{0,8},{4,12},{8,0},{12,4},{16,24},{20,28},{24,16},{28,20},{1,9},{5... | collective-permute-start | bytes 786440 | tf_op jit(solution)/shard_map/ppermute | solution.py:84
  139.1 113.6 %reduce-scatter.11.cloned.1.call-start = ((), (), s32[]{:S(2)}) async-start(), calls=%async_computation.11 | async-start | bytes 2969600 | tf_op jit(solution)/shard_map/reduce_scatter | solution.py:49
  142.2 13.5 %collective-permute-start.18 = (bf16[128,1024]{1,0:T(8,128)(2,1)S(1)}, bf16[128,1024]{1,0:T(8,128)(2,1)S(1)}, u32[]{:S(2)}, u32[]{:S(2)}) collective-permute-start(bf16[128,1024]{1,0:T(8,128)(2,1)S(1)} %collective-permute-done.17), channel_id=1, source_target_pairs={{0,4},{4,0},{8,12},{12,8},{16,20},{20,16},{24,28},{28,24},{1,5},{5... | collective-permute-start | bytes 786440 | tf_op jit(solution)/shard_map/ppermute | solution.py:84
  143.5 10.8 %collective-permute-start.12 = (bf16[128,1024]{1,0:T(8,128)(2,1)S(1)}, bf16[128,1024]{1,0:T(8,128)(2,1)S(1)}, u32[]{:S(2)}, u32[]{:S(2)}) collective-permute-start(bf16[128,1024]{1,0:T(8,128)(2,1)S(1)} %collective-permute-done.10), channel_id=1, source_target_pairs={{0,8},{4,12},{8,0},{12,4},{16,24},{20,28},{24,16},{28,20},{1,9},{5... | collective-permute-start | bytes 786440 | tf_op jit(solution)/shard_map/ppermute | solution.py:84
  144.7 13.9 %collective-permute-start.11 = (bf16[128,1024]{1,0:T(8,128)(2,1)S(1)}, bf16[128,1024]{1,0:T(8,128)(2,1)S(1)}, u32[]{:S(2)}, u32[]{:S(2)}) collective-permute-start(bf16[128,1024]{1,0:T(8,128)(2,1)S(1)} %collective-permute-done.10), channel_id=1, source_target_pairs={{0,4},{4,0},{8,12},{12,8},{16,20},{20,16},{24,28},{28,24},{1,5},{5... | collective-permute-start | bytes 786440 | tf_op jit(solution)/shard_map/ppermute | solution.py:84
  149.2 10.8 %collective-permute-start.20 = (bf16[128,1024]{1,0:T(8,128)(2,1)S(1)}, bf16[128,1024]{1,0:T(8,128)(2,1)S(1)}, u32[]{:S(2)}, u32[]{:S(2)}) collective-permute-start(bf16[128,1024]{1,0:T(8,128)(2,1)S(1)} %collective-permute-done.19), channel_id=1, source_target_pairs={{0,4},{4,0},{8,12},{12,8},{16,20},{20,16},{24,28},{28,24},{1,5},{5... | collective-permute-start | bytes 786440 | tf_op jit(solution)/shard_map/ppermute | solution.py:84
  206.2 99.2 %all-gather.13.cloned.1.call-start = ((), (), s32[]{:S(2)}) async-start(), calls=%async_computation.12 | async-start | bytes 2969600 | tf_op jit(solution)/shard_map/all_gather | solution.py:45
  255.0 105.1 %all-gather.15.cloned.1.call-start = ((), (), s32[]{:S(2)}) async-start(), calls=%async_computation.13 | async-start | bytes 2969600 | tf_op jit(solution)/shard_map/all_gather | solution.py:45
  256.1 10.3 %collective-permute-start.24 = (bf16[128,1024]{1,0:T(8,128)(2,1)}, bf16[128,1024]{1,0:T(8,128)(2,1)S(1)}, u32[]{:S(2)}, u32[]{:S(2)}) collective-permute-start(bf16[128,1024]{1,0:T(8,128)(2,1)} %pad_maximum_fusion.16), channel_id=1, source_target_pairs={{0,16},{4,20},{8,24},{12,28},{16,0},{20,4},{24,8},{28,12},{1,17},{... | collective-permute-start | bytes 786440 | tf_op jit(solution)/shard_map/ppermute | solution.py:84
  257.6 9.6 collective-permute-start.22
  266.9 9.7 collective-permute-start.25
  275.2 36.6 %collective-permute-start.27 = (bf16[128,1024]{1,0:T(8,128)(2,1)S(1)}, bf16[128,1024]{1,0:T(8,128)(2,1)S(1)}, u32[]{:S(2)}, u32[]{:S(2)}) collective-permute-start(bf16[128,1024]{1,0:T(8,128)(2,1)S(1)} %collective-permute-done.26), channel_id=1, source_target_pairs={{0,4},{4,0},{8,12},{12,8},{16,20},{20,16},{24,28},{28,24},{1,5},{5... | collective-permute-start | bytes 786440 | tf_op jit(solution)/shard_map/ppermute | solution.py:84
  311.0 99.0 %reduce-scatter.13.cloned.1.call-start = ((), (), s32[]{:S(2)}) async-start(), calls=%async_computation.14 | async-start | bytes 2969600 | tf_op jit(solution)/shard_map/reduce_scatter | solution.py:49
  363.4 98.9 %all-gather.17.cloned.1.call-start = ((), (), s32[]{:S(2)}) async-start(), calls=%async_computation.15 | async-start | bytes 2969600 | tf_op jit(solution)/shard_map/all_gather | solution.py:45
  364.4 51.0 %collective-permute-start.38 = (bf16[128,1024]{1,0:T(8,128)(2,1)S(1)}, bf16[128,1024]{1,0:T(8,128)(2,1)}, u32[]{:S(2)}, u32[]{:S(2)}) collective-permute-start(bf16[128,1024]{1,0:T(8,128)(2,1)S(1)} %copy-done.76), channel_id=1, source_target_pairs={{0,16},{4,20},{8,24},{12,28},{16,0},{20,4},{24,8},{28,12},{1,17},{... | collective-permute-start | bytes 786440 | tf_op jit(solution)/shard_map/ppermute | solution.py:84
  365.8 55.9 %collective-permute-start.36 = (bf16[128,1024]{1,0:T(8,128)(2,1)S(1)}, bf16[128,1024]{1,0:T(8,128)(2,1)}, u32[]{:S(2)}, u32[]{:S(2)}) collective-permute-start(bf16[128,1024]{1,0:T(8,128)(2,1)S(1)} %copy-done.76), channel_id=1, source_target_pairs={{0,8},{4,12},{8,0},{12,4},{16,24},{20,28},{24,16},{28,20},{1,9},{5... | collective-permute-start | bytes 786440 | tf_op jit(solution)/shard_map/ppermute | solution.py:84
  367.3 54.9 %collective-permute-start.35 = (bf16[128,1024]{1,0:T(8,128)(2,1)S(1)}, bf16[128,1024]{1,0:T(8,128)(2,1)}, u32[]{:S(2)}, u32[]{:S(2)}) collective-permute-start(bf16[128,1024]{1,0:T(8,128)(2,1)S(1)} %copy-done.76), channel_id=1, source_target_pairs={{0,4},{4,0},{8,12},{12,8},{16,20},{20,16},{24,28},{28,24},{1,5},{5... | collective-permute-start | bytes 786440 | tf_op jit(solution)/shard_map/ppermute | solution.py:84
  367.3 52.7 %collective-permute-start.29 = (bf16[128,1024]{1,0:T(8,128)(2,1)S(1)}, bf16[128,1024]{1,0:T(8,128)(2,1)}, u32[]{:S(2)}, u32[]{:S(2)}) collective-permute-start(bf16[128,1024]{1,0:T(8,128)(2,1)S(1)} %copy-done.77), channel_id=1, source_target_pairs={{0,8},{4,12},{8,0},{12,4},{16,24},{20,28},{24,16},{28,20},{1,9},{5... | collective-permute-start | bytes 786440 | tf_op jit(solution)/shard_map/ppermute | solution.py:84
  367.9 49.0 %collective-permute-start.28 = (bf16[128,1024]{1,0:T(8,128)(2,1)S(1)}, bf16[128,1024]{1,0:T(8,128)(2,1)}, u32[]{:S(2)}, u32[]{:S(2)}) collective-permute-start(bf16[128,1024]{1,0:T(8,128)(2,1)S(1)} %copy-done.77), channel_id=1, source_target_pairs={{0,4},{4,0},{8,12},{12,8},{16,20},{20,16},{24,28},{28,24},{1,5},{5... | collective-permute-start | bytes 786440 | tf_op jit(solution)/shard_map/ppermute | solution.py:84
  412.0 123.7 %reduce-scatter.15.cloned.1.call-start = ((), (), s32[]{:S(2)}) async-start(), calls=%async_computation.16 | async-start | bytes 3010560 | tf_op jit(solution)/shard_map/reduce_scatter | solution.py:69
  416.9 11.0 %collective-permute-start.40 = (bf16[128,1024]{1,0:T(8,128)(2,1)}, bf16[128,1024]{1,0:T(8,128)(2,1)S(1)}, u32[]{:S(2)}, u32[]{:S(2)}) collective-permute-start(bf16[128,1024]{1,0:T(8,128)(2,1)} %collective-permute-done.38), channel_id=1, source_target_pairs={{0,8},{4,12},{8,0},{12,4},{16,24},{20,28},{24,16},{28,20},{1,9},{5... | collective-permute-start | bytes 786440 | tf_op jit(solution)/shard_map/ppermute | solution.py:84
  420.0 16.7 %collective-permute-start.39 = (bf16[128,1024]{1,0:T(8,128)(2,1)}, bf16[128,1024]{1,0:T(8,128)(2,1)S(1)}, u32[]{:S(2)}, u32[]{:S(2)}) collective-permute-start(bf16[128,1024]{1,0:T(8,128)(2,1)} %collective-permute-done.38), channel_id=1, source_target_pairs={{0,4},{4,0},{8,12},{12,8},{16,20},{20,16},{24,28},{28,24},{1,5},{5... | collective-permute-start | bytes 786440 | tf_op jit(solution)/shard_map/ppermute | solution.py:84
  422.2 12.1 %collective-permute-start.37 = (bf16[128,1024]{1,0:T(8,128)(2,1)}, bf16[128,1024]{1,0:T(8,128)(2,1)S(1)}, u32[]{:S(2)}, u32[]{:S(2)}) collective-permute-start(bf16[128,1024]{1,0:T(8,128)(2,1)} %collective-permute-done.36), channel_id=1, source_target_pairs={{0,4},{4,0},{8,12},{12,8},{16,20},{20,16},{24,28},{28,24},{1,5},{5... | collective-permute-start | bytes 786440 | tf_op jit(solution)/shard_map/ppermute | solution.py:84
  488.4 102.2 %all-gather.19.cloned.1.call-start = ((), (), s32[]{:S(2)}) async-start(), calls=%async_computation.17 | async-start | bytes 2969600 | tf_op jit(solution)/shard_map/all_gather | solution.py:45
  540.2 99.1 %reduce-scatter.17.cloned.1.call-start = ((), (), s32[]{:S(2)}) async-start(), calls=%async_computation.18 | async-start | bytes 2969600 | tf_op jit(solution)/shard_map/reduce_scatter | solution.py:49
  590.6 122.8 %reduce-scatter.19.cloned.1.call-start = ((), (), s32[]{:S(2)}) async-start(), calls=%async_computation.19 | async-start | bytes 3010560 | tf_op jit(solution)/shard_map/reduce_scatter | solution.py:69
  665.0 104.8 %all-gather.21.cloned.1.call-start = ((), (), s32[]{:S(2)}) async-start(), calls=%async_computation.20 | async-start | bytes 2969600 | tf_op jit(solution)/shard_map/all_gather | solution.py:45
  719.4 115.9 %reduce-scatter.21.cloned.1.call-start = ((), (), s32[]{:S(2)}) async-start(), calls=%async_computation.21 | async-start | bytes 3010560 | tf_op jit(solution)/shard_map/reduce_scatter | solution.py:69
  732.2 9.3 collective-permute-start.66
  735.2 9.5 collective-permute-start.68
  738.4 52.8 %collective-permute-start.63 = (bf16[128,1024]{1,0:T(8,128)(2,1)S(1)}, bf16[128,1024]{1,0:T(8,128)(2,1)}, u32[]{:S(2)}, u32[]{:S(2)}) collective-permute-start(bf16[128,1024]{1,0:T(8,128)(2,1)S(1)} %get-tuple-element.204), channel_id=1, source_target_pairs={{0,4},{4,0},{8,12},{12,8},{16,20},{20,16},{24,28},{28,24},{1,5},{5... | collective-permute-start | bytes 786440 | tf_op jit(solution)/shard_map/ppermute | solution.py:84
  738.4 49.9 %collective-permute-start.80 = (bf16[128,1024]{1,0:T(8,128)(2,1)S(1)}, bf16[128,1024]{1,0:T(8,128)(2,1)}, u32[]{:S(2)}, u32[]{:S(2)}) collective-permute-start(bf16[128,1024]{1,0:T(8,128)(2,1)S(1)} %get-tuple-element.194), channel_id=1, source_target_pairs={{0,4},{4,0},{8,12},{12,8},{16,20},{20,16},{24,28},{28,24},{1,5},{5... | collective-permute-start | bytes 786440 | tf_op jit(solution)/shard_map/ppermute | solution.py:84
  738.9 53.8 %collective-permute-start.65 = (bf16[128,1024]{1,0:T(8,128)(2,1)}, bf16[128,1024]{1,0:T(8,128)(2,1)}, u32[]{:S(2)}, u32[]{:S(2)}) collective-permute-start(bf16[128,1024]{1,0:T(8,128)(2,1)} %get-tuple-element.208), channel_id=1, source_target_pairs={{0,8},{4,12},{8,0},{12,4},{16,24},{20,28},{24,16},{28,20},{1,9},{5... | collective-permute-start | bytes 786440 | tf_op jit(solution)/shard_map/ppermute | solution.py:84
  741.5 46.9 %collective-permute-start.82 = (bf16[128,1024]{1,0:T(8,128)(2,1)}, bf16[128,1024]{1,0:T(8,128)(2,1)}, u32[]{:S(2)}, u32[]{:S(2)}) collective-permute-start(bf16[128,1024]{1,0:T(8,128)(2,1)} %get-tuple-element.197), channel_id=1, source_target_pairs={{0,8},{4,12},{8,0},{12,4},{16,24},{20,28},{24,16},{28,20},{1,9},{5... | collective-permute-start | bytes 786440 | tf_op jit(solution)/shard_map/ppermute | solution.py:84
  745.9 46.8 %collective-permute-start.69 = (bf16[128,1024]{1,0:T(8,128)(2,1)S(1)}, bf16[128,1024]{1,0:T(8,128)(2,1)S(1)}, u32[]{:S(2)}, u32[]{:S(2)}) collective-permute-start(bf16[128,1024]{1,0:T(8,128)(2,1)S(1)} %add_convert_fusion.12), channel_id=1, source_target_pairs={{0,16},{4,20},{8,24},{12,28},{16,0},{20,4},{24,8},{28,12},{1,17},{... | collective-permute-start | bytes 786440 | tf_op jit(solution)/shard_map/ppermute | solution.py:84
  788.1 102.4 %all-gather.23.cloned.1.call-start = ((), (), s32[]{:S(2)}) async-start(), calls=%async_computation.22 | async-start | bytes 2969600 | tf_op jit(solution)/shard_map/all_gather | solution.py:45
  788.3 11.5 %collective-permute-start.77 = (bf16[128,1024]{1,0:T(8,128)(2,1)S(1)}, bf16[128,1024]{1,0:T(8,128)(2,1)S(1)}, u32[]{:S(2)}, u32[]{:S(2)}) collective-permute-start(bf16[128,1024]{1,0:T(8,128)(2,1)S(1)} %get-tuple-element.192), channel_id=1, source_target_pairs={{0,4},{4,0},{8,12},{12,8},{16,20},{20,16},{24,28},{28,24},{1,5},{5... | collective-permute-start | bytes 786440 | tf_op jit(solution)/shard_map/ppermute | solution.py:84
  788.4 11.5 %collective-permute-start.79 = (bf16[128,1024]{1,0:T(8,128)(2,1)S(1)}, bf16[128,1024]{1,0:T(8,128)(2,1)S(1)}, u32[]{:S(2)}, u32[]{:S(2)}) collective-permute-start(bf16[128,1024]{1,0:T(8,128)(2,1)S(1)} %get-tuple-element.196), channel_id=1, source_target_pairs={{0,8},{4,12},{8,0},{12,4},{16,24},{20,28},{24,16},{28,20},{1,9},{5... | collective-permute-start | bytes 786440 | tf_op jit(solution)/shard_map/ppermute | solution.py:84
  803.4 13.5 %collective-permute-start.49 = (bf16[128,1024]{0,1:T(8,128)(2,1)S(1)}, bf16[128,1024]{0,1:T(8,128)(2,1)}, u32[]{:S(2)}, u32[]{:S(2)}) collective-permute-start(bf16[128,1024]{0,1:T(8,128)(2,1)S(1)} %pad_maximum_fusion.21), channel_id=1, source_target_pairs={{0,4},{4,0},{8,12},{12,8},{16,20},{20,16},{24,28},{28,24},{1,5},{5... | collective-permute-start | bytes 786440 | tf_op jit(solution)/shard_map/ppermute | solution.py:84
  803.7 13.3 %collective-permute-start.51 = (bf16[128,1024]{0,1:T(8,128)(2,1)S(1)}, bf16[128,1024]{0,1:T(8,128)(2,1)}, u32[]{:S(2)}, u32[]{:S(2)}) collective-permute-start(bf16[128,1024]{0,1:T(8,128)(2,1)S(1)} %add_convert_fusion.28), channel_id=1, source_target_pairs={{0,8},{4,12},{8,0},{12,4},{16,24},{20,28},{24,16},{28,20},{1,9},{5... | collective-permute-start | bytes 786440 | tf_op jit(solution)/shard_map/ppermute | solution.py:84
  829.5 17.7 %collective-permute-start.60 = (bf16[128,1024]{1,0:T(8,128)(2,1)}, bf16[128,1024]{1,0:T(8,128)(2,1)}, u32[]{:S(2)}, u32[]{:S(2)}) collective-permute-start(bf16[128,1024]{1,0:T(8,128)(2,1)} %get-tuple-element.199), channel_id=1, source_target_pairs={{0,4},{4,0},{8,12},{12,8},{16,20},{20,16},{24,28},{28,24},{1,5},{5... | collective-permute-start | bytes 786440 | tf_op jit(solution)/shard_map/ppermute | solution.py:84
  829.5 30.3 %collective-permute-start.59 = (bf16[128,1024]{1,0:T(8,128)(2,1)}, bf16[128,1024]{1,0:T(8,128)(2,1)}, u32[]{:S(2)}, u32[]{:S(2)}) collective-permute-start(bf16[128,1024]{1,0:T(8,128)(2,1)} %get-tuple-element.200), channel_id=1, source_target_pairs={{0,4},{4,0},{8,12},{12,8},{16,20},{20,16},{24,28},{28,24},{1,5},{5... | collective-permute-start | bytes 786440 | tf_op jit(solution)/shard_map/ppermute | solution.py:84
  830.0 17.2 %collective-permute-start.57 = (bf16[128,1024]{1,0:T(8,128)(2,1)}, bf16[128,1024]{1,0:T(8,128)(2,1)}, u32[]{:S(2)}, u32[]{:S(2)}) collective-permute-start(bf16[128,1024]{1,0:T(8,128)(2,1)} %get-tuple-element.201), channel_id=1, source_target_pairs={{0,4},{4,0},{8,12},{12,8},{16,20},{20,16},{24,28},{28,24},{1,5},{5... | collective-permute-start | bytes 786440 | tf_op jit(solution)/shard_map/ppermute | solution.py:84
  840.0 145.6 %reduce-scatter.23.cloned.1.call-start = ((), (), s32[]{:S(2)}) async-start(), calls=%async_computation.23 | async-start | bytes 3010560 | tf_op jit(solution)/shard_map/reduce_scatter | solution.py:69
  846.7 10.0 collective-permute-start.74
  846.7 10.5 %collective-permute-start.71 = (bf16[128,1024]{1,0:T(8,128)(2,1)}, bf16[128,1024]{1,0:T(8,128)(2,1)}, u32[]{:S(2)}, u32[]{:S(2)}) collective-permute-start(bf16[128,1024]{1,0:T(8,128)(2,1)} %get-tuple-element.189), channel_id=1, source_target_pairs={{0,4},{4,0},{8,12},{12,8},{16,20},{20,16},{24,28},{28,24},{1,5},{5... | collective-permute-start | bytes 786440 | tf_op jit(solution)/shard_map/ppermute | solution.py:84
  849.4 11.9 %collective-permute-start.61 = (bf16[128,1024]{1,0:T(8,128)(2,1)}, bf16[128,1024]{1,0:T(8,128)(2,1)}, u32[]{:S(2)}, u32[]{:S(2)}) collective-permute-start(bf16[128,1024]{1,0:T(8,128)(2,1)} %get-tuple-element.203), channel_id=1, source_target_pairs={{0,8},{4,12},{8,0},{12,4},{16,24},{20,28},{24,16},{28,20},{1,9},{5... | collective-permute-start | bytes 786440 | tf_op jit(solution)/shard_map/ppermute | solution.py:84
  856.7 16.6 %collective-permute-start.56 = (bf16[128,1024]{1,0:T(8,128)(2,1)S(1)}, bf16[128,1024]{1,0:T(8,128)(2,1)S(1)}, u32[]{:S(2)}, u32[]{:S(2)}) collective-permute-start(bf16[128,1024]{1,0:T(8,128)(2,1)S(1)} %copy-done.78), channel_id=1, source_target_pairs={{0,4},{4,0},{8,12},{12,8},{16,20},{20,16},{24,28},{28,24},{1,5},{5... | collective-permute-start | bytes 786440 | tf_op jit(solution)/shard_map/ppermute | solution.py:84
  857.2 17.6 %collective-permute-start.58 = (bf16[128,1024]{1,0:T(8,128)(2,1)}, bf16[128,1024]{1,0:T(8,128)(2,1)S(1)}, u32[]{:S(2)}, u32[]{:S(2)}) collective-permute-start(bf16[128,1024]{1,0:T(8,128)(2,1)} %get-tuple-element.202), channel_id=1, source_target_pairs={{0,8},{4,12},{8,0},{12,4},{16,24},{20,28},{24,16},{28,20},{1,9},{5... | collective-permute-start | bytes 786440 | tf_op jit(solution)/shard_map/ppermute | solution.py:84
  859.8 11.6 %collective-permute-start.75 = (bf16[128,1024]{1,0:T(8,128)(2,1)}, bf16[128,1024]{1,0:T(8,128)(2,1)}, u32[]{:S(2)}, u32[]{:S(2)}) collective-permute-start(bf16[128,1024]{1,0:T(8,128)(2,1)} %get-tuple-element.191), channel_id=1, source_target_pairs={{0,8},{4,12},{8,0},{12,4},{16,24},{20,28},{24,16},{28,20},{1,9},{5... | collective-permute-start | bytes 786440 | tf_op jit(solution)/shard_map/ppermute | solution.py:84
  863.3 11.5 %collective-permute-start.62 = (bf16[128,1024]{1,0:T(8,128)(2,1)}, bf16[128,1024]{1,0:T(8,128)(2,1)S(1)}, u32[]{:S(2)}, u32[]{:S(2)}) collective-permute-start(bf16[128,1024]{1,0:T(8,128)(2,1)} %add_convert_fusion.18), channel_id=1, source_target_pairs={{0,16},{4,20},{8,24},{12,28},{16,0},{20,4},{24,8},{28,12},{1,17},{... | collective-permute-start | bytes 786440 | tf_op jit(solution)/shard_map/ppermute | solution.py:84
  864.8 12.8 %collective-permute-start.70 = (bf16[128,1024]{1,0:T(8,128)(2,1)S(1)}, bf16[128,1024]{1,0:T(8,128)(2,1)S(1)}, u32[]{:S(2)}, u32[]{:S(2)}) collective-permute-start(bf16[128,1024]{1,0:T(8,128)(2,1)S(1)} %copy-done.79), channel_id=1, source_target_pairs={{0,4},{4,0},{8,12},{12,8},{16,20},{20,16},{24,28},{28,24},{1,5},{5... | collective-permute-start | bytes 786440 | tf_op jit(solution)/shard_map/ppermute | solution.py:84
  953.2 14.2 %collective-permute-start.42 = (bf16[128,1024]{0,1:T(8,128)(2,1)S(1)}, bf16[128,1024]{0,1:T(8,128)(2,1)S(1)}, u32[]{:S(2)}, u32[]{:S(2)}) collective-permute-start(bf16[128,1024]{0,1:T(8,128)(2,1)S(1)} %pad_maximum_fusion.17), channel_id=1, source_target_pairs={{0,4},{4,0},{8,12},{12,8},{16,20},{20,16},{24,28},{28,24},{1,5},{5... | collective-permute-start | bytes 786440 | tf_op jit(solution)/shard_map/ppermute | solution.py:84
  953.4 14.0 %collective-permute-start.44 = (bf16[128,1024]{0,1:T(8,128)(2,1)S(1)}, bf16[128,1024]{0,1:T(8,128)(2,1)S(1)}, u32[]{:S(2)}, u32[]{:S(2)}) collective-permute-start(bf16[128,1024]{0,1:T(8,128)(2,1)S(1)} %add_convert_fusion.34), channel_id=1, source_target_pairs={{0,8},{4,12},{8,0},{12,4},{16,24},{20,28},{24,16},{28,20},{1,9},{5... | collective-permute-start | bytes 786440 | tf_op jit(solution)/shard_map/ppermute | solution.py:84
  (191 other events, 2301.0 us)
Sparse Core Ops, SparseCore 0:
  10.2 53.9 all-gather.8
  90.9 46.0 reduce-scatter.8
  139.2 50.1 all-gather.10
  206.3 46.3 reduce-scatter.10
  255.1 50.2 all-gather.12
  311.1 48.9 all-gather.14
  363.6 46.3 reduce-scatter.12
  412.1 50.2 all-gather.16
  488.5 47.0 reduce-scatter.14
  540.3 50.2 all-gather.18
  592.9 46.3 reduce-scatter.16
  665.1 48.3 reduce-scatter.18
  719.5 50.2 all-gather.20
  788.2 47.0 reduce-scatter.20
  840.1 50.2 all-gather.22
  938.5 47.0 reduce-scatter.22
